TPU v7x, 32 devices: a whole 2x2x4 slice. The times are simulated.
32 devices in a mesh: tensor: 4 (over z), dp: 4 (over y, x), ctx: 2 (over core).
Axes of the slice: x: 2, y: 2, z: 4, core: 2. Of those that a mesh axis runs over, the one named last changes fastest.
Arguments:
- tokens: bfloat16 [1024, 2048], P(('dp', 'ctx')), may hold values from -6 to 6
- cotangent: bfloat16 [1024, 2048], P(('dp', 'ctx')), may hold values from -6 to 6
- sequence_loops: int32 [4], P('dp'), may hold values from 0 to 1
- attention_gain: bfloat16 [2048], P(('dp', 'ctx')), may hold values from 0.099609375 to 1.8984375
- query_weight: bfloat16 [2048, 2048], P(('dp', 'ctx'), 'tensor'), may hold values from -0.125 to 0.125
- key_weight: bfloat16 [2048, 256], P(('dp', 'ctx')), may hold values from -0.125 to 0.125
- value_weight: bfloat16 [2048, 256], P(('dp', 'ctx')), may hold values from -0.125 to 0.125
- attention_output_weight: bfloat16 [2048, 2048], P('tensor', ('dp', 'ctx')), may hold values from -2 to 2
- lowrank_output_first: bfloat16 [2, 2048, 256], P(None, ('tensor', 'dp', 'ctx')), may hold values from -1.5 to 1.5
- lowrank_output_second: bfloat16 [2, 256, 2048], P(None, None, ('dp', 'ctx')), may hold values from -0.375 to 0.375
- feedforward_gain: bfloat16 [2048], P(('dp', 'ctx')), may hold values from 0.099609375 to 1.8984375
- gate_weight: bfloat16 [2048, 16384], P(('dp', 'ctx'), 'tensor'), may hold values from -0.125 to 0.125
- up_weight: bfloat16 [2048, 16384], P(('dp', 'ctx'), 'tensor'), may hold values from -0.125 to 0.125
- down_weight: bfloat16 [16384, 2048], P('tensor', ('dp', 'ctx')), may hold values from -0.046875 to 0.046875
- lowrank_down_first: bfloat16 [2, 16384, 256], P(None, ('tensor', 'dp', 'ctx')), may hold values from -0.046875 to 0.046875
- lowrank_down_second: bfloat16 [2, 256, 2048], P(None, None, ('dp', 'ctx')), may hold values from -0.375 to 0.375
Outputs:
- out: bfloat16 [1024, 2048], P(('dp', 'ctx'))
- input_grad: bfloat16 [1024, 2048], P(('dp', 'ctx'))
- grad_attn_gain: float32 [2048], P(('dp', 'ctx'))
- grad_w_query: float32 [2048, 2048], P(('dp', 'ctx'), 'tensor')
- grad_w_key: float32 [2048, 256], P(('dp', 'ctx'))
- grad_w_value: float32 [2048, 256], P(('dp', 'ctx'))
- grad_w_out: float32 [2048, 2048], P('tensor', ('dp', 'ctx'))
- grad_lora_out_a: float32 [2, 2048, 256], P(None, ('tensor', 'dp', 'ctx'))
- grad_lora_out_b: float32 [2, 256, 2048], P(None, None, ('dp', 'ctx'))
- grad_mlp_gain: float32 [2048], P(('dp', 'ctx'))
- grad_w_gate: float32 [2048, 16384], P(('dp', 'ctx'), 'tensor')
- grad_w_up: float32 [2048, 16384], P(('dp', 'ctx'), 'tensor')
- grad_w_down: float32 [16384, 2048], P('tensor', ('dp', 'ctx'))
- grad_lora_down_a: float32 [2, 16384, 256], P(None, ('tensor', 'dp', 'ctx'))
- grad_lora_down_b: float32 [2, 256, 2048], P(None, None, ('dp', 'ctx'))
All inputs are finite; a program needn't handle non-finite values.
Results may differ from a plain program's by a relative error of at most 0.015.
Values may be sent and summed in bfloat16 or wider, within the bound.
No kernel may reach another device: no remote copies, remote signals or barrier semaphores. Data moves between devices by JAX's collectives and lax.ppermute only.
A program may use at most 320 MiB of HBM per device.

v0:
```python
import jax
import jax.numpy as jnp
from jax import lax
from jax.sharding import PartitionSpec as P

HEAD_WIDTH = 256
LOOP_COUNT = 2


def rms_scale(values, gain_vec):
    inverse = lax.rsqrt(jnp.mean(values * values, axis=-1, keepdims=True) + 1e-06)
    unit_rows = values * inverse
    return (unit_rows, inverse, unit_rows * gain_vec)


def rms_back(grads, unit_rows, inverse, gain_vec):
    scaled = grads * gain_vec
    inner_mean = jnp.mean(scaled * unit_rows, axis=-1, keepdims=True)
    return (inverse * (scaled - unit_rows * inner_mean), jnp.sum(grads * unit_rows, axis=0))


def layout(loop_id, group_rows):
    positions = jnp.arange(group_rows, dtype=jnp.int32)
    loop_row = (jnp.arange(LOOP_COUNT, dtype=jnp.int32) == loop_id).astype(jnp.float32)
    select = jnp.zeros((group_rows, LOOP_COUNT), jnp.float32) + loop_row[None, :]
    return (positions, select)


def tables(offset):
    half_width = HEAD_WIDTH // 2
    frequency = 10000.0 ** (-(jnp.arange(half_width, dtype=jnp.float32) * 2.0 / HEAD_WIDTH))
    angles = offset.astype(jnp.float32)[:, None] * frequency[None, :]
    return (jnp.cos(angles), jnp.sin(angles))


def rotate(values, cosine, sine):
    half_width = values.shape[-1] // 2
    first_half = values[..., :half_width]
    second_half = values[..., half_width:]
    return jnp.concatenate(
        [first_half * cosine - second_half * sine, second_half * cosine + first_half * sine],
        axis=-1,
    )


def unrotate(grads, cosine, sine):
    half_width = grads.shape[-1] // 2
    first_half = grads[..., :half_width]
    second_half = grads[..., half_width:]
    return jnp.concatenate(
        [first_half * cosine + second_half * sine, second_half * cosine - first_half * sine],
        axis=-1,
    )


def gelu_product(gate_proj, up_proj):
    return jax.nn.gelu(gate_proj, approximate=True) * up_proj


def body(
    tokens,
    cotangent,
    sequence_loops,
    attention_gain,
    query_weight,
    key_weight,
    value_weight,
    attention_output_weight,
    lowrank_output_first,
    lowrank_output_second,
    feedforward_gain,
    gate_weight,
    up_weight,
    down_weight,
    lowrank_down_first,
    lowrank_down_second,
):
    gathered = (
        lax.all_gather(attention_gain, ("dp", "ctx"), axis=0, tiled=True),
        lax.all_gather(query_weight, ("dp", "ctx"), axis=0, tiled=True),
        lax.all_gather(key_weight, ("dp", "ctx"), axis=0, tiled=True),
        lax.all_gather(value_weight, ("dp", "ctx"), axis=0, tiled=True),
        lax.all_gather(attention_output_weight, ("dp", "ctx"), axis=1, tiled=True),
        lax.all_gather(lowrank_output_first, ("dp", "ctx"), axis=1, tiled=True),
        lax.all_gather(lowrank_output_second, ("dp", "ctx"), axis=2, tiled=True),
        lax.all_gather(feedforward_gain, ("dp", "ctx"), axis=0, tiled=True),
        lax.all_gather(gate_weight, ("dp", "ctx"), axis=0, tiled=True),
        lax.all_gather(up_weight, ("dp", "ctx"), axis=0, tiled=True),
        lax.all_gather(down_weight, ("dp", "ctx"), axis=1, tiled=True),
        lax.all_gather(lowrank_down_first, ("dp", "ctx"), axis=1, tiled=True),
        lax.all_gather(lowrank_down_second, ("dp", "ctx"), axis=2, tiled=True),
    )
    (
        gain_one,
        query_w,
        key_w,
        value_w,
        output_weight,
        output_first,
        output_second,
        gain_two,
        gate_w,
        up_w,
        down_w,
        down_a,
        down_b,
    ) = gathered
    gain_one_f = gain_one.astype(jnp.float32)
    gain_two_f = gain_two.astype(jnp.float32)
    row_count = tokens.shape[0]
    span_count = lax.axis_size("ctx")
    group_rows = row_count * span_count
    row_begin = lax.axis_index("ctx") * row_count
    positions, select = layout(sequence_loops[0], group_rows)
    cosine, sine = tables(positions)
    own_cos = lax.dynamic_slice_in_dim(cosine, row_begin, row_count, 0)
    own_sin = lax.dynamic_slice_in_dim(sine, row_begin, row_count, 0)
    own_pos = lax.dynamic_slice_in_dim(positions, row_begin, row_count, 0)
    own_select = lax.dynamic_slice_in_dim(select, row_begin, row_count, 0)
    selected_transposed = own_select.T[:, :, None]
    selected_lowrank = selected_transposed.astype(jnp.bfloat16)
    score_scale = HEAD_WIDTH ** (-0.5)
    inputs = tokens.astype(jnp.float32)
    unit_one, inverse_one, scaled_one = rms_scale(inputs, gain_one_f)
    normed = scaled_one.astype(jnp.bfloat16)
    queries = jnp.dot(normed, query_w, preferred_element_type=jnp.float32)
    keys_raw = jnp.dot(normed, key_w, preferred_element_type=jnp.float32)
    values_own = jnp.dot(normed, value_w, preferred_element_type=jnp.float32).astype(jnp.bfloat16)
    heads_local = query_w.shape[1] // HEAD_WIDTH
    query_rot = rotate(
        queries.reshape(row_count, heads_local, HEAD_WIDTH),
        own_cos[:, None, :],
        own_sin[:, None, :],
    ).astype(jnp.bfloat16)
    key_rot = rotate(keys_raw, own_cos, own_sin).astype(jnp.bfloat16)
    keys_all, values_all = (
        lax.all_gather(key_rot, "ctx", axis=0, tiled=True),
        lax.all_gather(values_own, "ctx", axis=0, tiled=True),
    )
    block_rows = min(512, row_count)
    block_count = row_count // block_rows

    def scores_for():
        raw_scores = (
            jnp.einsum("qhd,kd->hqk", query_rot, keys_all, preferred_element_type=jnp.float32)
            * score_scale
        )
        allowed = positions[None, :] <= own_pos[:, None]
        return (query_rot, jnp.where(allowed[None], raw_scores, -1e30))

    def forward_block(block_index):
        query_block, scores = scores_for()
        row_peak = jnp.max(scores, axis=-1, keepdims=True)
        exp_terms = jnp.exp(scores - row_peak)
        row_total = jnp.sum(exp_terms, axis=-1, keepdims=True)
        soft_weights = exp_terms / row_total
        block_out = jnp.einsum(
            "hqk,kd->qhd",
            soft_weights.astype(jnp.bfloat16),
            values_all,
            preferred_element_type=jnp.float32,
        )
        return (
            block_out.reshape(block_rows, heads_local * HEAD_WIDTH).astype(jnp.bfloat16),
            (row_peak + jnp.log(row_total))[..., 0],
        )

    mixed_blocks, log_totals = lax.map(forward_block, jnp.arange(block_count))
    heads_output = mixed_blocks.reshape(row_count, heads_local * HEAD_WIDTH)
    lowrank_summands = jnp.einsum(
        "wq,dqs->dws", heads_output, output_first, preferred_element_type=jnp.float32
    )
    lowrank_portion = jnp.sum(lowrank_summands * selected_transposed, axis=0)
    attention_part = jnp.dot(heads_output, output_weight, preferred_element_type=jnp.float32)
    attention_sum, lowrank_total_sum = lax.psum((attention_part, lowrank_portion), "tensor")
    lowrank_masked = lowrank_total_sum.astype(jnp.bfloat16)[None] * selected_lowrank
    resid = inputs + (
        attention_sum
        + jnp.einsum(
            "ivn,inj->vj", lowrank_masked, output_second, preferred_element_type=jnp.float32
        )
    )
    unit_two, inverse_two, scaled_two = rms_scale(resid, gain_two_f)
    normed_two = scaled_two.astype(jnp.bfloat16)
    gate_proj = jnp.dot(normed_two, gate_w, preferred_element_type=jnp.float32)
    up_proj = jnp.dot(normed_two, up_w, preferred_element_type=jnp.float32)
    activated, gelu_pullback = jax.vjp(gelu_product, gate_proj, up_proj)
    inner_act = activated.astype(jnp.bfloat16)
    mid_terms = jnp.einsum("tf,lfr->ltr", inner_act, down_a, preferred_element_type=jnp.float32)
    mid_part = jnp.sum(mid_terms * selected_transposed, axis=0)
    mlp_part = jnp.dot(inner_act, down_w, preferred_element_type=jnp.float32)
    mlp_sum, mid_sum = lax.psum((mlp_part, mid_part), "tensor")
    mid_masked = mid_sum.astype(jnp.bfloat16)[None] * selected_lowrank
    outputs = (
        resid
        + (
            mlp_sum
            + jnp.einsum("ivn,inj->vj", mid_masked, down_b, preferred_element_type=jnp.float32)
        )
    ).astype(jnp.bfloat16)
    down_grad_w = jnp.einsum("tf,td->fd", inner_act, cotangent, preferred_element_type=jnp.float32)
    mid_grad = jnp.sum(
        jnp.einsum("td,lrd->ltr", cotangent, down_b, preferred_element_type=jnp.float32)
        * selected_transposed,
        axis=0,
    ).astype(jnp.bfloat16)
    mid_grad_masked = mid_grad[None] * selected_lowrank
    down_a_grad = jnp.einsum(
        "tf,ltr->lfr", inner_act, mid_grad_masked, preferred_element_type=jnp.float32
    )
    inner_grad = jnp.einsum(
        "td,fd->tf", cotangent, down_w, preferred_element_type=jnp.float32
    ) + jnp.einsum("ltr,lfr->tf", mid_grad_masked, down_a, preferred_element_type=jnp.float32)
    gate_grad, up_grad = gelu_pullback(inner_grad)
    gate_low = gate_grad.astype(jnp.bfloat16)
    up_low = up_grad.astype(jnp.bfloat16)
    gate_grad_w = jnp.einsum("td,tf->df", normed_two, gate_low, preferred_element_type=jnp.float32)
    up_grad_w = jnp.einsum("td,tf->df", normed_two, up_low, preferred_element_type=jnp.float32)
    normed_two_part = jnp.einsum(
        "tf,df->td", gate_low, gate_w, preferred_element_type=jnp.float32
    ) + jnp.einsum("tf,df->td", up_low, up_w, preferred_element_type=jnp.float32)
    normed_two_grad = lax.psum(normed_two_part, "tensor")
    resid_delta, gain_two_grad = rms_back(normed_two_grad, unit_two, inverse_two, gain_two_f)
    resid_grad = cotangent.astype(jnp.float32) + resid_delta
    residual_lowrank = resid_grad.astype(jnp.bfloat16)
    down_b_grad = jnp.einsum(
        "azu,zy->auy", mid_masked, cotangent, preferred_element_type=jnp.float32
    )
    out_grad_w = jnp.einsum(
        "tc,td->cd", heads_output, residual_lowrank, preferred_element_type=jnp.float32
    )
    out_b_grad = jnp.einsum(
        "azu,zy->auy", lowrank_masked, residual_lowrank, preferred_element_type=jnp.float32
    )
    lowrank_gradient = jnp.sum(
        jnp.einsum(
            "td,lrd->ltr", residual_lowrank, output_second, preferred_element_type=jnp.float32
        )
        * selected_transposed,
        axis=0,
    ).astype(jnp.bfloat16)
    lowrank_gradient_masked = lowrank_gradient[None] * selected_lowrank
    out_a_grad = jnp.einsum(
        "mi,nmu->niu", heads_output, lowrank_gradient_masked, preferred_element_type=jnp.float32
    )
    heads_grad = (
        jnp.einsum("td,cd->tc", residual_lowrank, output_weight, preferred_element_type=jnp.float32)
        + jnp.einsum(
            "dng,dag->na", lowrank_gradient_masked, output_first, preferred_element_type=jnp.float32
        )
    ).astype(jnp.bfloat16)
    heads_grad_split = heads_grad.reshape(row_count, heads_local, HEAD_WIDTH)

    def backward_block(carried, block_index):
        key_acc, value_acc = carried
        query_block, scores = scores_for()
        soft_weights = jnp.exp(scores - log_totals[block_index][..., None])
        soft_grad = jnp.einsum(
            "qhd,kd->hqk", heads_grad_split, values_all, preferred_element_type=jnp.float32
        )
        row_dot = jnp.sum(soft_grad * soft_weights, axis=-1, keepdims=True)
        score_grad = (soft_weights * (soft_grad - row_dot)).astype(jnp.bfloat16) * score_scale
        query_part = jnp.einsum(
            "hqk,kd->qhd", score_grad, keys_all, preferred_element_type=jnp.float32
        )
        key_acc = key_acc + jnp.einsum(
            "hqk,qhd->kd", score_grad, query_block, preferred_element_type=jnp.float32
        )
        value_acc = value_acc + jnp.einsum(
            "hqk,qhd->kd",
            soft_weights.astype(jnp.bfloat16),
            heads_grad_split,
            preferred_element_type=jnp.float32,
        )
        return ((key_acc, value_acc), query_part)

    zero_grads = jnp.zeros((group_rows, HEAD_WIDTH), jnp.float32)
    (key_grad_all, value_grad_all), query_parts = lax.scan(
        backward_block, (zero_grads, zero_grads), jnp.arange(block_count)
    )
    query_rot_grad = query_parts.reshape(row_count, heads_local, HEAD_WIDTH)
    query_low = (
        unrotate(query_rot_grad, own_cos[:, None, :], own_sin[:, None, :])
        .reshape(row_count, heads_local * HEAD_WIDTH)
        .astype(jnp.bfloat16)
    )
    key_grad_all = unrotate(key_grad_all, cosine, sine)
    key_own, value_own = (
        lax.psum_scatter(key_grad_all, "ctx", scatter_dimension=0, tiled=True),
        lax.psum_scatter(value_grad_all, "ctx", scatter_dimension=0, tiled=True),
    )
    key_total, value_total = lax.psum((key_own, value_own), "tensor")
    key_low = key_total.astype(jnp.bfloat16)
    value_low = value_total.astype(jnp.bfloat16)
    query_grad_w = jnp.einsum("td,tc->dc", normed, query_low, preferred_element_type=jnp.float32)
    key_grad_w = jnp.einsum("td,tc->dc", normed, key_low, preferred_element_type=jnp.float32)
    value_grad_w = jnp.einsum("td,tc->dc", normed, value_low, preferred_element_type=jnp.float32)
    normed_part = jnp.einsum("tc,dc->td", query_low, query_w, preferred_element_type=jnp.float32)
    normed_sum = lax.psum(normed_part, "tensor")
    normed_grad = (
        normed_sum
        + jnp.einsum("tc,dc->td", key_low, key_w, preferred_element_type=jnp.float32)
        + jnp.einsum("tc,dc->td", value_low, value_w, preferred_element_type=jnp.float32)
    )
    input_delta, gain_one_grad = rms_back(normed_grad, unit_one, inverse_one, gain_one_f)
    input_grad = (resid_grad + input_delta).astype(jnp.bfloat16)
    every_grad = (
        lax.psum_scatter(gain_one_grad, ("dp", "ctx"), scatter_dimension=0, tiled=True),
        lax.psum_scatter(query_grad_w, ("dp", "ctx"), scatter_dimension=0, tiled=True),
        lax.psum_scatter(key_grad_w, ("dp", "ctx"), scatter_dimension=0, tiled=True),
        lax.psum_scatter(value_grad_w, ("dp", "ctx"), scatter_dimension=0, tiled=True),
        lax.psum_scatter(out_grad_w, ("dp", "ctx"), scatter_dimension=1, tiled=True),
        lax.psum_scatter(out_a_grad, ("dp", "ctx"), scatter_dimension=1, tiled=True),
        lax.psum_scatter(out_b_grad, ("dp", "ctx"), scatter_dimension=2, tiled=True),
        lax.psum_scatter(gain_two_grad, ("dp", "ctx"), scatter_dimension=0, tiled=True),
        lax.psum_scatter(gate_grad_w, ("dp", "ctx"), scatter_dimension=0, tiled=True),
        lax.psum_scatter(up_grad_w, ("dp", "ctx"), scatter_dimension=0, tiled=True),
        lax.psum_scatter(down_grad_w, ("dp", "ctx"), scatter_dimension=1, tiled=True),
        lax.psum_scatter(down_a_grad, ("dp", "ctx"), scatter_dimension=1, tiled=True),
        lax.psum_scatter(down_b_grad, ("dp", "ctx"), scatter_dimension=2, tiled=True),
    )
    (
        grad_gain_one,
        grad_query,
        grad_key,
        grad_value,
        grad_out,
        grad_out_a,
        grad_out_b,
        grad_gain_two,
        grad_gate,
        grad_up,
        grad_down,
        grad_down_a,
        grad_down_b,
    ) = every_grad
    return (
        outputs,
        input_grad,
        grad_gain_one,
        grad_query,
        grad_key,
        grad_value,
        grad_out,
        grad_out_a,
        grad_out_b,
        grad_gain_two,
        grad_gate,
        grad_up,
        grad_down,
        grad_down_a,
        grad_down_b,
    )


def solution(mesh):
    placed = (
        P(("dp", "ctx"), None),
        P(("dp", "ctx"), None),
        P("dp"),
        P(("dp", "ctx")),
        P(("dp", "ctx"), "tensor"),
        P(("dp", "ctx"), None),
        P(("dp", "ctx"), None),
        P("tensor", ("dp", "ctx")),
        P(None, ("tensor", "dp", "ctx"), None),
        P(None, None, ("dp", "ctx")),
        P(("dp", "ctx")),
        P(("dp", "ctx"), "tensor"),
        P(("dp", "ctx"), "tensor"),
        P("tensor", ("dp", "ctx")),
        P(None, ("tensor", "dp", "ctx"), None),
        P(None, None, ("dp", "ctx")),
    )
    return jax.shard_map(
        body,
        mesh=mesh,
        in_specs=placed,
        out_specs=(
            P(("dp", "ctx"), None),
            P(("dp", "ctx"), None),
            P(("dp", "ctx")),
            P(("dp", "ctx"), "tensor"),
            P(("dp", "ctx"), None),
            P(("dp", "ctx"), None),
            P("tensor", ("dp", "ctx")),
            P(None, ("tensor", "dp", "ctx"), None),
            P(None, None, ("dp", "ctx")),
            P(("dp", "ctx")),
            P(("dp", "ctx"), "tensor"),
            P(("dp", "ctx"), "tensor"),
            P("tensor", ("dp", "ctx")),
            P(None, ("tensor", "dp", "ctx"), None),
            P(None, None, ("dp", "ctx")),
        ),
        check_vma=False,
    )
```

profile of v0, /device:TPU:0, one launch (start us, length us, event | category | flops | bytes accessed | tf_op | source)
XLA Modules:
  0.0 1834.9 jit_solution(1765877652037449067)
XLA Ops:
  11.9 10.4 all-gather
  24.2 11.8 all-gather.13.cloned.1.call-done
  39.5 21.8 %all-gather.15.cloned.1.call-done = bf16[2048,256]{1,0:T(8,128)(2,1)} async-done(((bf16[256,256]{1,0:T(8,128)(2,1)}), bf16[2048,256]{1,0:T(8,128)(2,1)}) %all-gather.15.cloned.1.call-update) | async-done | bytes 1048592 | tf_op jit(solution)/shard_map/all_gather | solution.py:81
  64.9 26.1 %all-gather.17.cloned.1.call-done = bf16[2048,512]{1,0:T(8,128)(2,1)} async-done(((bf16[256,512]{1,0:T(8,128)(2,1)}), bf16[2048,512]{1,0:T(8,128)(2,1)}) %all-gather.17.cloned.1.call-update) | async-done | bytes 2097168 | tf_op jit(solution)/shard_map/all_gather | solution.py:80
  94.1 26.8 %all-gather.19.cloned.1.call-done = bf16[512,2048]{1,0:T(8,128)(2,1)} async-done(((bf16[512,256]{1,0:T(8,128)(2,1)}), bf16[512,2048]{1,0:T(8,128)(2,1)}) %all-gather.19.cloned.1.call-update) | async-done | bytes 2097168 | tf_op jit(solution)/shard_map/all_gather | solution.py:83
  136.5 10.3 all_gather.52
  147.0 21.6 %all-reduce.20 = bf16[128,256]{1,0:T(8,128)(2,1)S(1)} all-reduce(f32[128,256]{1,0:T(8,128)S(1)} %fusion.22), channel_id=1, replica_groups=mesh['tensor'=4,'dp'=4,'ctx'=2] {'tensor'}, use_global_device_ids=true, to_apply=%region_5.6 | all-reduce | flops 32768 | bytes 196608 | tf_op jit(solution)/shard_map/psum | solution.py:175
  181.3 54.9 %all-reduce.13.cloned.1.call-done = f32[128,2048]{1,0:T(8,128)} async-done(((f32[128,2048]{1,0:T(8,128)}), f32[128,2048]{1,0:T(8,128)}) %all-reduce.13.cloned.1.call-update) | async-done | bytes 1048592 | tf_op jit(solution)/shard_map/psum | solution.py:175
  238.9 88.2 %all-gather.25.cloned.1.call-done = bf16[2048,4096]{1,0:T(8,128)(2,1)} async-done(((bf16[256,4096]{1,0:T(8,128)(2,1)}), bf16[2048,4096]{1,0:T(8,128)(2,1)}) %all-gather.25.cloned.1.call-update) | async-done | bytes 16777232 | tf_op jit(solution)/shard_map/all_gather | solution.py:88
  336.6 82.2 %all-gather.23.cloned.1.call-done = bf16[2048,4096]{1,0:T(8,128)(2,1)} async-done(((bf16[256,4096]{1,0:T(8,128)(2,1)}), bf16[2048,4096]{1,0:T(8,128)(2,1)}) %all-gather.23.cloned.1.call-update) | async-done | bytes 16777232 | tf_op jit(solution)/shard_map/all_gather | solution.py:87
  428.2 85.3 %all-gather.27.cloned.1.call-done = bf16[4096,2048]{1,0:T(8,128)(2,1)} async-done(((bf16[4096,256]{1,0:T(8,128)(2,1)}), bf16[4096,2048]{1,0:T(8,128)(2,1)}) %all-gather.27.cloned.1.call-update) | async-done | bytes 16777232 | tf_op jit(solution)/shard_map/all_gather | solution.py:89
  513.6 12.7 fusion.122
  526.2 25.8 %all-gather.29.cloned.1.call-done = bf16[2,4096,256]{2,1,0:T(8,128)(2,1)} async-done(((bf16[2,512,256]{2,1,0:T(8,128)(2,1)}), bf16[2,4096,256]{2,1,0:T(8,128)(2,1)}) %all-gather.29.cloned.1.call-update) | async-done | bytes 4194320 | tf_op jit(solution)/shard_map/all_gather | solution.py:90
  559.9 13.2 fusion.123
  573.2 12.9 convolution_add_fusion.2
  586.8 51.4 %all-reduce.15.cloned.1.call-done = f32[128,2048]{1,0:T(8,128)} async-done(((f32[128,2048]{1,0:T(8,128)}), f32[128,2048]{1,0:T(8,128)}) %all-reduce.15.cloned.1.call-update) | async-done | bytes 1048592 | tf_op jit(solution)/shard_map/psum | solution.py:222
  682.8 25.8 %all-reduce.21 = (bf16[128,256]{1,0:T(8,128)(2,1)}, bf16[128,256]{1,0:T(8,128)(2,1)}, bf16[128,256]{1,0:T(8,128)(2,1)}) all-reduce(f32[128,256]{1,0:T(8,128)S(1)} %fusion.27, f32[128,256]{1,0:T(8,128)} %reduce-scatter.13.cloned.1.call-done, ...), channel_id=1, replica_groups=mesh['tensor'=4,'dp'=4,'ctx'=2] {'tensor'}, use_global_device_ids=true, to_apply=%region_9.10 | all-reduce | flops 98304 | bytes 589824 | tf_op jit(solution)/shard_map/psum | solution.py:192
  729.4 14.5 fusion.128
  745.1 13.4 fusion.127
  759.7 13.3 fusion.126
  777.2 38.8 %all-reduce.19.cloned.1.call-done = (f32[128,2048]{1,0:T(8,128)}, f32[128,2048]{1,0:T(8,128)}) async-done(((f32[128,2048]{1,0:T(8,128)}, f32[128,2048]{1,0:T(8,128)}), (f32[128,2048]{1,0:T(8,128)}, f32[128,2048]{1,0:T(8,128)})) %all-reduce.19.cloned.1.call-update) | async-done | bytes 2097168 | tf_op jit(solution)/shard_map/psum | solution.py:192
  818.6 23.6 %all-reduce.3 = (f32[2048]{0:T(1024)S(1)}, f32[2048]{0:T(1024)S(1)}) all-reduce(f32[2048]{0:T(1024)S(1)} %get-tuple-element.119, f32[2048]{0:T(1024)S(1)} %copy-done.30), channel_id=4, replica_groups=mesh['tensor'=4,'dp'=4,'ctx'=2] {'dp','ctx'}, use_global_device_ids=true, to_apply=%region_22.23.clone | all-reduce | flops 4096 | bytes 32768
  848.4 41.4 %reduce-scatter.33.cloned.1.call-done = f32[2,512,256]{1,2,0:T(8,128)} async-done(((f32[2,4096,256]{1,2,0:T(8,128)}), f32[2,512,256]{1,2,0:T(8,128)}) %reduce-scatter.33.cloned.1.call-update) | async-done | bytes 1048592 | tf_op jit(solution)/shard_map/reduce_scatter | solution.py:319
  892.3 42.3 %reduce-scatter.21.cloned.1.call-done = f32[256,256]{1,0:T(8,128)} async-done(((f32[2048,256]{1,0:T(8,128)}), f32[256,256]{1,0:T(8,128)}) %reduce-scatter.21.cloned.1.call-update) | async-done | bytes 262160 | tf_op jit(solution)/shard_map/reduce_scatter | solution.py:311
  934.6 45.0 %reduce-scatter.19.cloned.1.call-done = f32[256,256]{1,0:T(8,128)} async-done(((f32[2048,256]{1,0:T(8,128)}), f32[256,256]{1,0:T(8,128)}) %reduce-scatter.19.cloned.1.call-update) | async-done | bytes 262160 | tf_op jit(solution)/shard_map/reduce_scatter | solution.py:310
  979.6 55.0 %reduce-scatter.17.cloned.1.call-done = f32[256,512]{1,0:T(8,128)} async-done(((f32[2048,512]{1,0:T(8,128)}), f32[256,512]{1,0:T(8,128)}) %reduce-scatter.17.cloned.1.call-update) | async-done | bytes 524304 | tf_op jit(solution)/shard_map/reduce_scatter | solution.py:309
  1034.6 55.0 %reduce-scatter.25.cloned.1.call-done = f32[2,256,256]{2,1,0:T(8,128)} async-done(((f32[2,256,2048]{2,1,0:T(8,128)}), f32[2,256,256]{2,1,0:T(8,128)}) %reduce-scatter.25.cloned.1.call-update) | async-done | bytes 524304 | tf_op jit(solution)/shard_map/reduce_scatter | solution.py:314
  1089.6 55.0 %reduce-scatter.23.cloned.1.call-done = f32[512,256]{1,0:T(8,128)} async-done(((f32[512,2048]{1,0:T(8,128)}), f32[512,256]{1,0:T(8,128)}) %reduce-scatter.23.cloned.1.call-update) | async-done | bytes 524304 | tf_op jit(solution)/shard_map/reduce_scatter | solution.py:312
  1144.6 55.0 %reduce-scatter.35.cloned.1.call-done = f32[2,256,256]{2,1,0:T(8,128)} async-done(((f32[2,256,2048]{2,1,0:T(8,128)}), f32[2,256,256]{2,1,0:T(8,128)}) %reduce-scatter.35.cloned.1.call-update) | async-done | bytes 524304 | tf_op jit(solution)/shard_map/reduce_scatter | solution.py:320
  1199.7 209.3 %reduce-scatter.31.cloned.1.call-done = f32[4096,256]{1,0:T(8,128)} async-done(((f32[4096,2048]{1,0:T(8,128)}), f32[4096,256]{1,0:T(8,128)}) %reduce-scatter.31.cloned.1.call-update) | async-done | bytes 4194320 | tf_op jit(solution)/shard_map/reduce_scatter | solution.py:318
  1409.0 209.6 %reduce-scatter.29.cloned.1.call-done = f32[256,4096]{1,0:T(8,128)} async-done(((f32[2048,4096]{1,0:T(8,128)}), f32[256,4096]{1,0:T(8,128)}) %reduce-scatter.29.cloned.1.call-update) | async-done | bytes 4194320 | tf_op jit(solution)/shard_map/reduce_scatter | solution.py:317
  1618.6 209.5 %reduce-scatter.27.cloned.1.call-done = f32[256,4096]{1,0:T(8,128)} async-done(((f32[2048,4096]{1,0:T(8,128)}), f32[256,4096]{1,0:T(8,128)}) %reduce-scatter.27.cloned.1.call-update) | async-done | bytes 4194320 | tf_op jit(solution)/shard_map/reduce_scatter | solution.py:316
  (245 shorter events, 155.6 us)
Async XLA Ops:
  7.2 28.8 %all-gather.13.cloned.1.call-start = ((), (), s32[]{:S(2)}) async-start(), calls=%async_computation.12 | async-start | bytes 1179648 | tf_op jit(solution)/shard_map/all_gather | solution.py:82
  7.9 53.4 %all-gather.15.cloned.1.call-start = ((), (), s32[]{:S(2)}) async-start(), calls=%async_computation.13 | async-start | bytes 1179648 | tf_op jit(solution)/shard_map/all_gather | solution.py:81
  8.7 82.3 %all-gather.17.cloned.1.call-start = ((), (), s32[]{:S(2)}) async-start(), calls=%async_computation.14 | async-start | bytes 2359296 | tf_op jit(solution)/shard_map/all_gather | solution.py:80
  9.4 111.5 %all-gather.19.cloned.1.call-start = ((), (), s32[]{:S(2)}) async-start(), calls=%async_computation.15 | async-start | bytes 2359296 | tf_op jit(solution)/shard_map/all_gather | solution.py:83
  10.0 158.8 %all-gather.31.cloned.1.call-start = ((), (), s32[]{:S(2)}) async-start(), calls=%async_computation.22 | async-start | bytes 2359296 | tf_op jit(solution)/shard_map/all_gather | solution.py:91
  10.6 170.8 %all-gather.21.cloned.1.call-start = ((), (), s32[]{:S(2)}) async-start(), calls=%async_computation.17 | async-start | bytes 2359296 | tf_op jit(solution)/shard_map/all_gather | solution.py:85
  11.1 225.1 %all-reduce.13.cloned.1.call-start = ((), (), s32[]{:S(2)}) async-start(), calls=%async_computation.16 | async-start | bytes 2097152 | tf_op jit(solution)/shard_map/psum | solution.py:175
  23.6 67.4 %copy-start.36 = (f32[128]{0:T(128)}, f32[128]{0:T(128)S(1)}, u32[]{:S(2)}) copy-start(f32[128]{0:T(128)S(1)} %add_rsqrt_fusion.1) | copy-start | bytes 1540
  124.0 203.2 %all-gather.25.cloned.1.call-start = ((), (), s32[]{:S(2)}) async-start(), calls=%async_computation.19 | async-start | bytes 18874368 | tf_op jit(solution)/shard_map/all_gather | solution.py:88
  124.7 294.0 %all-gather.23.cloned.1.call-start = ((), (), s32[]{:S(2)}) async-start(), calls=%async_computation.18 | async-start | bytes 18874368 | tf_op jit(solution)/shard_map/all_gather | solution.py:87
  125.5 388.1 %all-gather.27.cloned.1.call-start = ((), (), s32[]{:S(2)}) async-start(), calls=%async_computation.20 | async-start | bytes 18874368 | tf_op jit(solution)/shard_map/all_gather | solution.py:89
  126.1 426.0 %all-gather.29.cloned.1.call-start = ((), (), s32[]{:S(2)}) async-start(), calls=%async_computation.21 | async-start | bytes 4718592 | tf_op jit(solution)/shard_map/all_gather | solution.py:90
  126.8 511.4 %all-reduce.15.cloned.1.call-start = ((), (), s32[]{:S(2)}) async-start(), calls=%async_computation.23 | async-start | bytes 2097152 | tf_op jit(solution)/shard_map/psum | solution.py:222
  136.4 99.8 %copy-start.31 = (bf16[2]{0:T(256)(128)(2,1)}, bf16[2]{0:T(256)(128)(2,1)S(1)}, u32[]{:S(2)}) copy-start(bf16[2]{0:T(256)(128)(2,1)S(1)} %fusion.105) | copy-start | bytes 16
  168.7 70.0 %copy-start.15 = (bf16[128,256]{0,1:T(8,128)(2,1)}, bf16[128,256]{0,1:T(8,128)(2,1)S(1)}, u32[]{:S(2)}) copy-start(bf16[128,256]{0,1:T(8,128)(2,1)S(1)} %copy.79) | copy-start | bytes 196612
  171.1 381.0 %copy-start.20 = (bf16[256,128]{1,0:T(8,128)(2,1)}, bf16[256,128]{1,0:T(8,128)(2,1)S(1)}, u32[]{:S(2)}) copy-start(bf16[256,128]{1,0:T(8,128)(2,1)S(1)} %fusion.23) | copy-start | bytes 196612
  238.8 401.7 %copy-start.41 = (f32[128]{0:T(128)}, f32[128]{0:T(128)S(1)}, u32[]{:S(2)}) copy-start(f32[128]{0:T(128)S(1)} %add_rsqrt_fusion) | copy-start | bytes 1540
  428.2 123.9 %copy-start.32 = (bf16[2]{0:T(256)(128)(2,1)S(1)}, bf16[2]{0:T(256)(128)(2,1)}, u32[]{:S(2)}) copy-start(bf16[2]{0:T(256)(128)(2,1)} %copy-done.31) | copy-start | bytes 16
  586.1 96.6 %reduce-scatter.15.cloned.1.call-start = ((), (), s32[]{:S(2)}) async-start(), calls=%async_computation.25 | async-start | bytes 393216 | tf_op jit(solution)/shard_map/reduce_scatter | solution.py:290
  648.7 34.0 %reduce-scatter.13.cloned.1.call-start = ((), (), s32[]{:S(2)}) async-start(), calls=%async_computation.24 | async-start | bytes 393216 | tf_op jit(solution)/shard_map/reduce_scatter | solution.py:289
  655.1 120.6 %all-reduce.17.cloned.1.call-start = ((), (), s32[]{:S(2)}) async-start(), calls=%async_computation.36 | async-start | bytes 2097152
  670.3 145.7 %all-reduce.19.cloned.1.call-start = ((), (), s32[]{:S(2)}) async-start(), calls=%async_computation.37 | async-start | bytes 4194304 | tf_op jit(solution)/shard_map/psum | solution.py:192
  675.0 214.7 %reduce-scatter.33.cloned.1.call-start = ((), (), s32[]{:S(2)}) async-start(), calls=%async_computation.34 | async-start | bytes 9437184 | tf_op jit(solution)/shard_map/reduce_scatter | solution.py:319
  679.7 254.9 %reduce-scatter.21.cloned.1.call-start = ((), (), s32[]{:S(2)}) async-start(), calls=%async_computation.28 | async-start | bytes 2359296 | tf_op jit(solution)/shard_map/reduce_scatter | solution.py:311
  711.3 268.3 %reduce-scatter.19.cloned.1.call-start = ((), (), s32[]{:S(2)}) async-start(), calls=%async_computation.27 | async-start | bytes 2359296 | tf_op jit(solution)/shard_map/reduce_scatter | solution.py:310
  713.3 321.3 %reduce-scatter.17.cloned.1.call-start = ((), (), s32[]{:S(2)}) async-start(), calls=%async_computation.26 | async-start | bytes 4718592 | tf_op jit(solution)/shard_map/reduce_scatter | solution.py:309
  716.2 373.4 %reduce-scatter.25.cloned.1.call-start = ((), (), s32[]{:S(2)}) async-start(), calls=%async_computation.30 | async-start | bytes 4718592 | tf_op jit(solution)/shard_map/reduce_scatter | solution.py:314
  720.8 423.9 %reduce-scatter.23.cloned.1.call-start = ((), (), s32[]{:S(2)}) async-start(), calls=%async_computation.29 | async-start | bytes 4718592 | tf_op jit(solution)/shard_map/reduce_scatter | solution.py:312
  724.6 475.1 %reduce-scatter.35.cloned.1.call-start = ((), (), s32[]{:S(2)}) async-start(), calls=%async_computation.35 | async-start | bytes 4718592 | tf_op jit(solution)/shard_map/reduce_scatter | solution.py:320
  729.3 679.6 %reduce-scatter.31.cloned.1.call-start = ((), (), s32[]{:S(2)}) async-start(), calls=%async_computation.33 | async-start | bytes 37748736 | tf_op jit(solution)/shard_map/reduce_scatter | solution.py:318
  743.9 874.7 %reduce-scatter.29.cloned.1.call-start = ((), (), s32[]{:S(2)}) async-start(), calls=%async_computation.32 | async-start | bytes 37748736 | tf_op jit(solution)/shard_map/reduce_scatter | solution.py:317
  758.5 1069.6 %reduce-scatter.27.cloned.1.call-start = ((), (), s32[]{:S(2)}) async-start(), calls=%async_computation.31 | async-start | bytes 37748736 | tf_op jit(solution)/shard_map/reduce_scatter | solution.py:316
  (48 other events, 725.5 us)
Sparse Core Ops, SparseCore 0:
  9.9 26.0 all-gather.12
  37.9 23.3 all-gather.14
  63.2 27.7 all-gather.16
  92.7 28.0 all-gather.18
  122.6 28.8 all-gather.30
  153.2 28.0 all-gather.20
  184.3 51.8 all-reduce.12
  238.1 88.9 all-gather.24
  329.0 89.7 all-gather.22
  420.5 93.0 all-gather.26
  515.5 36.5 all-gather.28
  586.2 51.8 all-reduce.14
  648.8 7.0 reduce-scatter.14
  658.5 8.8 reduce-scatter.12
  670.4 57.8 all-reduce.16
  730.6 85.4 all-reduce.18
  819.3 70.3 reduce-scatter.32
  893.5 41.0 reduce-scatter.20
  938.4 41.1 reduce-scatter.18
  983.4 51.1 reduce-scatter.16
  1038.5 51.0 reduce-scatter.24
  1093.5 51.0 reduce-scatter.22
  1148.6 51.0 reduce-scatter.34
  1203.7 205.2 reduce-scatter.30
  1413.1 205.4 reduce-scatter.28
  1622.6 205.4 reduce-scatter.26
where the time goes:
time: 1840 us; the launch traced here: 1830 us
  waiting for transfers between devices  1510 us (82%)
  matrix products  179 us (10%)
  blocking collectives  104 us (6%)
    reduce_scatter x1, waiting for transfers between devices, body(): lax.psum_scatter(up_grad_w, ('dp', 'ctx'), scatter_dimension=0, tiled=True)  210 us
    reduce_scatter x1, waiting for transfers between devices, body(): lax.psum_scatter(gate_grad_w, ('dp', 'ctx'), scatter_dimension=0, tiled=T...  209 us
    reduce_scatter x1, waiting for transfers between devices, body(): lax.psum_scatter(down_grad_w, ('dp', 'ctx'), scatter_dimension=1, tiled=T...  209 us
    all_gather x1, waiting for transfers between devices, body(): lax.all_gather(up_weight, ('dp', 'ctx'), axis=0, tiled=True)  88.2 us
    all_gather x1, waiting for transfers between devices, body(): lax.all_gather(down_weight, ('dp', 'ctx'), axis=1, tiled=True)  85.3 us
    all_gather x1, waiting for transfers between devices, body(): lax.all_gather(gate_weight, ('dp', 'ctx'), axis=0, tiled=True)  82.2 us
    reduce_scatter x1, waiting for transfers between devices, body(): lax.psum_scatter(down_b_grad, ('dp', 'ctx'), scatter_dimension=2, tiled=T...  55 us
    reduce_scatter x1, waiting for transfers between devices, body(): lax.psum_scatter(out_b_grad, ('dp', 'ctx'), scatter_dimension=2, tiled=True)  55 us
  transfers between devices with their start and end apart: 26, of which 22 were waited for; matrix products, arithmetic and copies ran while one was open for 8% of the time, Pallas kernels for 0%

commit v1 on v0

v1 whole, which is shorter than its diff:
```python
import jax
import jax.numpy as jnp
from jax import lax
from jax.experimental import pallas as pl
from jax.experimental.pallas import tpu as pltpu
from jax.sharding import PartitionSpec as P


HEAD_WIDTH = 256
F32 = jnp.float32
BF16 = jnp.bfloat16


def dot(left, right, dims):
    return lax.dot_general(left, right, (dims, ((), ())), preferred_element_type=F32)


def mm(left, right):
    return dot(left, right, ((1,), (0,)))


def mm_nt(left, right):
    return dot(left, right, ((1,), (1,)))


def mm_tn(left, right):
    return dot(left, right, ((0,), (0,)))


def after(value, *tokens):
    return lax.optimization_barrier((value, *tokens))[0]


def cat(values, axis=0):
    return jnp.concatenate(values, axis=axis) if len(values) > 1 else values[0]


def rotate(values, cosine, sine):
    half = HEAD_WIDTH // 2
    first, second = values[..., :half], values[..., half:]
    return jnp.concatenate([first * cosine - second * sine, second * cosine + first * sine], axis=-1)


def rms_stats(values):
    inverse = lax.rsqrt(jnp.mean(values * values, axis=-1, keepdims=True) + 1e-06)
    return values * inverse, inverse


def rms_back(grads, unit_rows, inverse, gain):
    scaled = grads * gain
    return inverse * (scaled - unit_rows * jnp.mean(scaled * unit_rows, axis=-1, keepdims=True))


def shuffle(scalars, ins, outs, moves):
    count = len(ins)

    def place_of(spec, step, ref):
        return pl.multiple_of(spec(ref), step) if callable(spec) else spec

    def kernel(scalar_ref, *refs):
        for i, r, nr, c, ncol, o, ro, co, mask in moves:
            source = refs[count - i - 1] if i < 0 else refs[i]
            target = refs[count + o]
            row, col = place_of(r, nr, scalar_ref), place_of(c, ncol, scalar_ref)
            row_out, col_out = place_of(ro, nr, scalar_ref), place_of(co, ncol, scalar_ref)
            keep = None if mask is None else mask(scalar_ref)
            chunk = nr
            for size in (64, 32, 16):
                if nr % size == 0 and nr > size:
                    chunk = size
                    break

            def copy(step, row=row, col=col, row_out=row_out, col_out=col_out, keep=keep,
                     source=source, target=target, chunk=chunk, ncol=ncol):
                base = step * chunk
                if chunk % 16 == 0 and not isinstance(base, int):
                    base = pl.multiple_of(base, chunk)
                value = source[pl.ds(row + base, chunk), pl.ds(col, ncol)].astype(target.dtype)
                if keep is not None:
                    value = jnp.where(keep, value, jnp.zeros_like(value))
                target[pl.ds(row_out + base, chunk), pl.ds(col_out, ncol)] = value

            if chunk == nr:
                copy(0)
            else:
                pl.loop(0, nr // chunk)(copy)

    touched = sum(v.size * v.dtype.itemsize for v in list(ins)) + sum(
        o.size * o.dtype.itemsize for o in outs
    )
    return pl.pallas_call(
        kernel,
        out_shape=tuple(outs),
        in_specs=[pl.BlockSpec(memory_space=pltpu.SMEM)]
        + [pl.BlockSpec(memory_space=pltpu.VMEM)] * count,
        out_specs=tuple(pl.BlockSpec(memory_space=pltpu.VMEM) for _ in outs),
        cost_estimate=pl.CostEstimate(flops=0, bytes_accessed=touched, transcendentals=0),
    )(scalars, *ins)


def body(
    tokens,
    cotangent,
    sequence_loops,
    attention_gain,
    query_weight,
    key_weight,
    value_weight,
    attention_output_weight,
    lowrank_output_first,
    lowrank_output_second,
    feedforward_gain,
    gate_weight,
    up_weight,
    down_weight,
    lowrank_down_first,
    lowrank_down_second,
):
    nt, nd, nc = (lax.axis_size(name) for name in ("tensor", "dp", "ctx"))
    assert nc == 2
    ti, di, ci = (lax.axis_index(name) for name in ("tensor", "dp", "ctx"))
    rows, width = tokens.shape
    seq = rows * nc
    sub = rows // nt
    total = seq * nd
    loops, rank = lowrank_output_second.shape[:2]
    own_cols = width // (nd * nc)
    hidden = gate_weight.shape[1]
    fb = hidden // (nd * nc)
    head_cols = query_weight.shape[1]
    split = head_cols // HEAD_WIDTH >= nc
    qf = head_cols // nc if split else head_cols
    nh = qf // HEAD_WIDTH
    first_core = ci == 0
    spots = [(s, k) for k in range(nc) for s in range(nd)]

    def swap(value):
        return lax.ppermute(value, "ctx", [(i, i ^ 1) for i in range(nc)])

    def dperm(value, s):
        return lax.ppermute(value, "dp", [(i, i ^ s) for i in range(nd)]) if s else value

    def tperm(value, s):
        return lax.ppermute(value, "tensor", [(i, i ^ s) for i in range(nt)])

    def send(value, s, k):
        if s == 0:
            return swap(value) if k else value
        if k == 0:
            return dperm(value, s)
        pairs = [(i, i ^ (s * nc + k)) for i in range(nd * nc)]
        return lax.ppermute(value, ("dp", "ctx"), pairs)

    def pick(zero, one):
        return jnp.where(first_core, zero, one)

    def mine_of(value, axis):
        zero, one = jnp.split(value, 2, axis=axis)
        return pick(zero, one)

    def other_of(value, axis):
        zero, one = jnp.split(value, 2, axis=axis)
        return pick(one, zero)

    def pair(mine, other, axis):
        return pick(
            jnp.concatenate([mine, other], axis=axis), jnp.concatenate([other, mine], axis=axis)
        )

    def spread(pieces):
        got = [list(pieces)]
        if nd == 4:
            got.append([dperm(v, 1) for v in pieces])
            got.append([dperm(v, 2) for v in pieces])
            if len(pieces) == 1:
                half = pieces[0].shape[0] // 2
                got.append([dperm(got[1][0][:half], 2), dperm(got[2][0][half:], 1)])
            else:
                last = []
                for i in range(len(pieces)):
                    last.append(dperm(got[1][i], 2) if i % 2 == 0 else dperm(got[2][i], 1))
                got.append(last)
        else:
            for s in range(1, nd):
                got.append([dperm(v, s) for v in pieces])
        return got

    def spread_both(pieces):
        own = spread(pieces)
        return [own, [[swap(v) for v in group] for group in own]]

    def flat(groups):
        return [v for group in groups for v in group]

    def gather_t(value):
        return cat([value] + [tperm(value, z) for z in range(1, nt)])

    def reduce_t(value):
        step = value.shape[0] // nt
        own = value[:step]
        for z in range(1, nt):
            own = own + tperm(value[z * step : (z + 1) * step].astype(BF16), z).astype(F32)
        return own

    def reduce_c(own, other_low):
        return own + swap(other_low).astype(F32)

    def reduce_d(chip):
        got = []
        for s in range(1, nd):
            got.append(dperm(chip[s * rows : (s + 1) * rows].astype(BF16), s))
        return chip[:rows], got

    def total_of(own, got):
        for value in got:
            own = own + value.astype(F32)
        return own

    scalars = jnp.stack([ti, di, ci]).astype(jnp.int32)

    def block_of(s, k, size):
        return lambda ref: ((ref[1] ^ s) * nc + (ref[2] ^ k)) * size

    def masked(value, row_loops):
        return jnp.concatenate(
            [jnp.where(row_loops == l, value, jnp.zeros_like(value)) for l in range(loops)], axis=1
        )

    if split:
        q_zero, q_one = query_weight[:, :qf], query_weight[:, qf:]
    else:
        q_zero = q_one = query_weight
    for_zero = jnp.concatenate([q_zero, key_weight], axis=1)
    for_one = jnp.concatenate([q_one, value_weight], axis=1)
    w_cols = qf + HEAD_WIDTH
    gain_rows = jnp.concatenate([attention_gain, feedforward_gain])
    gain_rows = jnp.pad(gain_rows, (0, 15 * w_cols - gain_rows.shape[0])).reshape(15, w_cols)
    loop_row = jnp.broadcast_to(sequence_loops.astype(BF16)[:, None], (1, w_cols))
    gain_rows = jnp.concatenate([gain_rows, loop_row], axis=0)
    one_mine = jnp.concatenate([pick(for_zero, for_one), gain_rows], axis=0)
    one_got = swap(jnp.concatenate([pick(for_one, for_zero), gain_rows], axis=0))
    one_pieces = spread([one_mine, one_got])

    def z_block(z):
        return lambda ref: (ref[0] ^ z) * sub

    tok_rel, cot_rel = shuffle(
        scalars,
        [tokens, after(cotangent, one_got)],
        [jax.ShapeDtypeStruct(tokens.shape, BF16)] * 2,
        [
            (i, z_block(z), sub, 0, width, i, z * sub, 0, None)
            for i in range(2)
            for z in range(nt)
        ],
    )
    tok_seq = jnp.concatenate([tok_rel, swap(tok_rel)], axis=0)
    cot_t = cat([dperm(cot_rel[:sub], s) for s in range(nd)])
    cot_own = [cot_t] + [tperm(cot_t, z) for z in range(1, nt)]

    gu_out = shuffle(
        scalars,
        [after(gate_weight, one_got), up_weight],
        [jax.ShapeDtypeStruct((own_cols, 2 * fb), BF16)] * (nd * nc),
        [
            (g, 0, own_cols, block_of(s, k, fb), fb, j, 0, g * fb, None)
            for j, (s, k) in enumerate(spots)
            for g in range(2)
        ],
    )

    moves = []
    for s in range(nd):
        for k in range(nc):
            i = s * nc + k
            moves.append((i, 0, own_cols, 0, w_cols, 0, block_of(s, k, own_cols), 0, None))
            for g in range(2):
                at = g * own_cols
                moves.append(
                    (i, own_cols + at // w_cols, 1, at % w_cols, own_cols, 1, g,
                     block_of(s, k, own_cols), None)
                )
        moves.append((s * nc, own_cols + 15, 1, 0, 128, 1, 2, s * 128, None))
    w_one, gains = shuffle(
        scalars,
        flat(one_pieces),
        [
            jax.ShapeDtypeStruct((width, w_cols), BF16),
            jax.ShapeDtypeStruct((8, width), F32),
        ],
        moves,
    )
    gain_one, gain_two = gains[0:1], gains[1:2]
    loop_rel = gains[2, : nd * 128].reshape(nd, 128)[:, 0].astype(jnp.int32)
    scalars = jnp.concatenate([scalars, loop_rel])
    row_loop = jnp.broadcast_to(loop_rel[None, :, None], (nc, nd, rows)).reshape(total, 1)
    seq_loop = jnp.broadcast_to(loop_rel[:, None], (nd, seq)).reshape(total, 1)

    if split:
        o_mine = mine_of(attention_output_weight, 0)
        o_other = other_of(attention_output_weight, 0)
    else:
        o_mine = o_other = attention_output_weight
    o_rows = o_mine.shape[0]
    a_rows = lowrank_output_first.shape[1]
    groups = rank // own_cols
    o_both = jnp.concatenate([o_mine, swap(o_other)], axis=0)
    o_both = after(o_both, one_pieces[-1][-1])
    o_all = [o_both] + [dperm(o_both, s) for s in range(1, nd)]
    low_out = shuffle(
        scalars,
        [
            lowrank_output_second.reshape(loops * rank, own_cols),
            lowrank_down_second.reshape(loops * rank, own_cols),
            lowrank_output_first.reshape(loops * a_rows, rank),
        ],
        [jax.ShapeDtypeStruct((2 * rank + groups * a_rows, own_cols), BF16)] * nd,
        [
            (i, lambda ref, s=s: ref[3 + s] * rank, rank, 0, own_cols, s, i * rank, 0, None)
            for s in range(nd)
            for i in range(2)
        ]
        + [
            (2, lambda ref, s=s: ref[3 + s] * a_rows, a_rows, g * own_cols, own_cols, s,
             2 * rank + g * a_rows, 0, None)
            for s in range(nd)
            for g in range(groups)
        ],
    )
    low_own = [dperm(v, s) for s, v in enumerate(low_out)]
    low_all = low_own + [swap(v) for v in low_own]
    moves = []
    for s in range(nd):
        for k in range(nc):
            col = block_of(s, k, own_cols)
            moves.append((s, k * o_rows, o_rows, 0, own_cols, 0, 0, col, None))
            i = nd + k * nd + s
            moves.append((i, 0, rank, 0, own_cols, 1, 0, col, None))
            moves.append((i, rank, rank, 0, own_cols, 2, 0, col, None))
            for g in range(groups):
                moves.append(
                    (i, 2 * rank + g * a_rows, a_rows, 0, own_cols, 3,
                     block_of(s, k, a_rows), g * own_cols, None)
                )
    head_row = (lambda ref: ref[2] * qf) if split else 0
    moves.append((-4, head_row, qf, 0, rank, 0, 0, width, None))
    wo_cat, out_second, down_second, _ = shuffle(
        scalars,
        o_all + low_all,
        [
            jax.ShapeDtypeStruct((o_rows, width + rank), BF16),
            jax.ShapeDtypeStruct((rank, width), BF16),
            jax.ShapeDtypeStruct((rank, width), BF16),
            jax.ShapeDtypeStruct((head_cols, rank), BF16),
        ],
        moves,
    )

    gu_got = [
        send(after(v, o_all[-1], low_own[-1]) if s else v, s, k)
        for v, (s, k) in zip(gu_out, spots)
    ]

    own_rows = jnp.concatenate(
        [(ti ^ z) * sub + jnp.arange(sub, dtype=jnp.int32) for z in range(nt)]
    )
    positions = jnp.concatenate([ci * rows + own_rows, (1 - ci) * rows + own_rows])
    half_width = HEAD_WIDTH // 2
    frequency = 10000.0 ** (-(jnp.arange(half_width, dtype=F32) * 2.0 / HEAD_WIDTH))
    angles = positions.astype(F32)[:, None] * frequency[None, :]
    cosine, sine = jnp.cos(angles), jnp.sin(angles)
    allowed = positions[None, :] <= positions[:, None]
    score_scale = HEAD_WIDTH ** (-0.5)
    unit_one, inverse_one = rms_stats(tok_seq.astype(F32))
    normed_one = (unit_one * gain_one).astype(BF16)
    projected = mm(normed_one, w_one)
    kv_raw = projected[:, qf:]
    kv_own = pick(rotate(kv_raw, cosine, sine), kv_raw).astype(BF16)
    kv_other = swap_rows = swap(kv_own)
    kv_other = jnp.concatenate([swap_rows[rows:], swap_rows[:rows]], axis=0)
    key_rot, values = pick(kv_own, kv_other), pick(kv_other, kv_own)
    heads, softs, query_rots = [], [], []
    for h in range(nh):
        query_rot = rotate(
            projected[:, h * HEAD_WIDTH : (h + 1) * HEAD_WIDTH], cosine, sine
        ).astype(BF16)
        scores = jnp.where(allowed, mm_nt(query_rot, key_rot) * score_scale, -1e30)
        exp_terms = jnp.exp(scores - jnp.max(scores, axis=-1, keepdims=True))
        soft = exp_terms / jnp.sum(exp_terms, axis=-1, keepdims=True)
        heads.append(mm(soft.astype(BF16), values).astype(BF16))
        softs.append(soft)
        query_rots.append(query_rot)
    heads_out = cat(heads, 1)

    def for_rows(value):
        if split:
            return value
        return jnp.concatenate([value[:rows], jnp.zeros_like(value[rows:])], axis=0)

    summed = for_rows(heads_out)
    part_other = mm(summed[rows:], wo_cat).astype(BF16)
    part_own = mm(summed[:rows], wo_cat)
    attention_sum = reduce_t(part_own + swap(part_other).astype(F32))
    lora_mid = attention_sum[:, width:].astype(BF16)
    own_tokens = tok_rel[:sub].astype(F32)
    resid = own_tokens + attention_sum[:, :width] + mm(lora_mid, out_second)
    unit_two, inverse_two = rms_stats(resid)
    normed_two = (unit_two * gain_two).astype(BF16)
    two_t = gather_t(jnp.concatenate([normed_two, lora_mid], axis=1))
    two_pieces = spread_both([two_t])
    ins, moves = [], []
    for k in range(nc):
        for s in range(nd):
            at = 0
            for piece in two_pieces[k][s]:
                height = piece.shape[0]
                moves.append(
                    (len(ins), 0, height, 0, width, 0, (k * nd + s) * rows + at, 0, None)
                )
                moves.append(
                    (len(ins), 0, height, width, rank, 1, (s * nc + k) * rows + at, 0, None)
                )
                ins.append(piece)
                at += height
    normed_all, lora_mid_all = shuffle(
        scalars,
        ins,
        [
            jax.ShapeDtypeStruct((total, width), BF16),
            jax.ShapeDtypeStruct((total, rank), BF16),
        ],
        moves,
    )

    gu_got = [after(v, two_t) for v in gu_got]
    (gu_w,) = shuffle(
        scalars,
        gu_got,
        [jax.ShapeDtypeStruct((width, 2 * fb), BF16)],
        [
            (j, 0, own_cols, 0, 2 * fb, 0, block_of(s, k, own_cols), 0, None)
            for j, (s, k) in enumerate(spots)
        ],
    )
    down_out = shuffle(
        scalars,
        [after(down_weight, one_got)],
        [jax.ShapeDtypeStruct((fb, own_cols), BF16)] * (nd * nc),
        [
            (0, block_of(s, k, fb), fb, 0, own_cols, j, 0, 0, None)
            for j, (s, k) in enumerate(spots)
        ],
    )
    down_got = [
        send(after(v, *two_pieces[0][-1]) if s else v, s, k)
        for v, (s, k) in zip(down_out, spots)
    ]
    cat_cols = width + loops * rank
    (down_cat,) = shuffle(
        scalars,
        down_got + [lowrank_down_first[l] for l in range(loops)],
        [jax.ShapeDtypeStruct((fb, cat_cols), BF16)],
        [
            (j, 0, fb, 0, own_cols, 0, 0, block_of(s, k, own_cols), None)
            for j, (s, k) in enumerate(spots)
        ]
        + [
            (nd * nc + l, 0, fb, 0, rank, 0, 0, width + l * rank, None) for l in range(loops)
        ],
    )

    mid_grad_own = mm_nt(after(cot_rel, two_t), down_second).astype(BF16)
    mg_own = cat([dperm(mid_grad_own, s) for s in range(nd)])
    mg_pieces = [mg_own, swap(mg_own)]
    cot_all = cot_own + [swap(v) for v in cot_own]
    moves = []
    for k in range(nc):
        for s in range(nd):
            for z in range(nt):
                moves.append(
                    (k * nt + z, s * sub, sub, 0, width, 0, (k * nd + s) * rows + z * sub, 0, None)
                )
            for l in range(loops):
                moves.append(
                    (nc * nt + k, s * rows, rows, 0, rank, 0, (k * nd + s) * rows,
                     width + l * rank, lambda ref, s=s, l=l: ref[3 + s] == l)
                )
    (cot_cat,) = shuffle(
        scalars, cot_all + mg_pieces, [jax.ShapeDtypeStruct((total, cat_cols), BF16)], moves
    )

    gate_up = mm(normed_all, gu_w)
    gate, up = gate_up[:, :fb], gate_up[:, fb:]
    root = (2.0 / jnp.pi) ** 0.5
    inside = jnp.tanh(root * (gate + 0.044715 * gate * gate * gate))
    gelu = 0.5 * gate * (1.0 + inside)
    slope = 0.5 * (1.0 + inside) + 0.5 * gate * (1.0 - inside * inside) * root * (
        1.0 + 3.0 * 0.044715 * gate * gate
    )
    inner = (gelu * up).astype(BF16)
    inner_grad = mm_nt(cot_cat, down_cat)
    gu_grad = jnp.concatenate(
        [(inner_grad * up * slope).astype(BF16), (inner_grad * gelu).astype(BF16)], axis=1
    )
    half_total = total // 2
    two_other = mm_nt(gu_grad[half_total:], gu_w).astype(BF16)
    two_own = mm_nt(gu_grad[:half_total], gu_w)
    two_chip, two_got = reduce_d(reduce_c(two_own, two_other))
    normed_two_grad = reduce_t(total_of(two_chip, two_got))
    inner, gu_grad = after((inner, gu_grad), two_own)

    def mlp_rows(lo, hi):
        product = mm(inner[lo:hi], down_cat)
        middle = product[:, width : width + rank]
        for l in range(1, loops):
            middle = jnp.where(
                row_loop[lo:hi] == l,
                product[:, width + l * rank : width + (l + 1) * rank],
                middle,
            )
        return jnp.concatenate([product[:, :width], middle], axis=1)

    mlp_other = mlp_rows(half_total, total).astype(BF16)
    mlp_own = mlp_rows(0, half_total)
    mlp_chip = reduce_c(mlp_own, mlp_other)
    mlp_chip, mlp_got = reduce_d(after(mlp_chip, *two_got))

    gu_grad_w = mm_tn(normed_all, gu_grad).astype(BF16)
    gu_grid = gu_grad_w.reshape(nd * nc, own_cols, 2 * fb)
    gu_back = []
    for s, k in spots:
        value = lax.dynamic_index_in_dim(gu_grid, (di ^ s) * nc + (ci ^ k), 0, keepdims=False)
        gu_back.append(send(after(value, *mlp_got) if s else value, s, k))
    grad_gate, grad_up = shuffle(
        scalars,
        gu_back,
        [jax.ShapeDtypeStruct((own_cols, hidden), F32)] * 2,
        [
            (j, 0, own_cols, g * fb, fb, g, 0, block_of(s, k, fb), None)
            for j, (s, k) in enumerate(spots)
            for g in range(2)
        ],
    )
    down_grad_cat = mm_tn(inner, cot_cat)
    down_deal = shuffle(
        scalars,
        [down_grad_cat],
        [jax.ShapeDtypeStruct((fb, own_cols), BF16)] * (nd * nc)
        + [jax.ShapeDtypeStruct((loops * fb, rank), F32)],
        [
            (0, 0, fb, block_of(s, k, own_cols), own_cols, j, 0, 0, None)
            for j, (s, k) in enumerate(spots)
        ]
        + [
            (0, 0, fb, width + l * rank, rank, nd * nc, l * fb, 0, None) for l in range(loops)
        ],
    )
    grad_down_a = down_deal[-1].reshape(loops, fb, rank)
    down_back = [send(after(v, *mlp_got) if s else v, s, k) for v, (s, k) in zip(down_deal, spots)]
    (grad_down,) = shuffle(
        scalars,
        down_back,
        [jax.ShapeDtypeStruct((nd * nc * fb, own_cols), F32)],
        [
            (j, 0, fb, 0, own_cols, 0, block_of(s, k, fb), 0, None)
            for j, (s, k) in enumerate(spots)
        ],
    )
    (cot_block,) = shuffle(
        scalars,
        [cot_cat],
        [jax.ShapeDtypeStruct((total, own_cols), BF16)],
        [(0, 0, total, block_of(0, 0, own_cols), own_cols, 0, 0, 0, None)],
    )
    own_cot = cot_rel[:sub].astype(F32)
    resid_grad = own_cot + rms_back(normed_two_grad, unit_two, inverse_two, gain_two)
    gain_two_part = jnp.sum(normed_two_grad * unit_two, axis=0)
    low_rows = gather_t(resid_grad.astype(BF16))
    resid_low = jnp.concatenate([low_rows, swap(low_rows)], axis=0)
    lora_mid_grad = mm_nt(resid_low, out_second).astype(BF16)
    low_cat = jnp.concatenate([resid_low, lora_mid_grad], axis=1)
    heads_grad = mm_nt(low_cat, wo_cat).astype(BF16)

    query_lows = []
    key_sum = value_sum = 0.0
    for h in range(nh):
        head_grad = heads_grad[:, h * HEAD_WIDTH : (h + 1) * HEAD_WIDTH]
        soft_grad = mm_nt(head_grad, values)
        row_dot = jnp.sum(soft_grad * softs[h], axis=-1, keepdims=True)
        score_grad = (softs[h] * (soft_grad - row_dot)).astype(BF16) * score_scale
        score_grad = score_grad.astype(BF16)
        query_lows.append(rotate(mm(score_grad, key_rot), cosine, -sine).astype(BF16))
        key_sum = key_sum + mm_tn(score_grad, query_rots[h])
        value_sum = value_sum + mm_tn(softs[h].astype(BF16), head_grad)
    query_low = cat(query_lows, 1)
    key_part = rotate(key_sum, cosine, -sine)
    kv_sum = pick(key_part, value_sum)
    if split:
        passed = swap(pick(value_sum, key_part).astype(BF16)).astype(F32)
        kv_sum = kv_sum + jnp.concatenate([passed[rows:], passed[:rows]], axis=0)
    grads_one = jnp.concatenate([for_rows(query_low), kv_sum.astype(BF16)], axis=1)
    one_other = mm_nt(grads_one[rows:], w_one)
    one_own = mm_nt(grads_one[:rows], w_one)
    gain_one_part = jnp.sum(one_own * unit_one[:rows], axis=0) + jnp.sum(
        one_other * unit_one[rows:], axis=0
    )
    normed_one_grad = reduce_t(reduce_c(one_own, one_other.astype(BF16)))
    mlp_sum = total_of(mlp_chip, [after(v, one_own) for v in mlp_got])
    mid_low = mlp_sum[:, width:].astype(BF16)
    mid_all = mlp_sum[:, width:]
    for z in range(1, nt):
        mid_z = tperm(mid_low, z).reshape(nt, sub, rank)
        mid_z = jnp.stack([mid_z[y ^ z] for y in range(nt)]).reshape(rows, rank)
        mid_all = mid_all + mid_z.astype(F32)
    mid_all = mid_all.astype(BF16)
    mlp_own = reduce_t(mlp_sum[:, :width])
    out_own = (resid + mlp_own + mm(mid_all[:sub], down_second)).astype(BF16)
    down_mid_own = cat([dperm(mid_all, s) for s in range(nd)])
    down_mid_all = jnp.concatenate([down_mid_own, swap(down_mid_own)], axis=0)
    grad_down_b = mm_tn(masked(down_mid_all, row_loop), cot_block)
    grad_down_b = grad_down_b.reshape(loops, rank, own_cols)
    input_own = resid_grad + rms_back(
        normed_one_grad, unit_one[:sub], inverse_one[:sub], gain_one
    )

    def rows_home(value):
        pieces = [value] + [tperm(value, z) for z in range(1, nt)]
        (placed,) = shuffle(
            scalars,
            pieces,
            [jax.ShapeDtypeStruct((rows, width), BF16)],
            [(z, 0, sub, 0, width, 0, z_block(z), 0, None) for z in range(nt)],
        )
        return placed

    outputs = rows_home(out_own)
    input_grad = rows_home(input_own.astype(BF16))

    def columns_for(value, extra):
        more = extra.shape[1]
        sent = shuffle(
            scalars,
            [value, extra],
            [jax.ShapeDtypeStruct((seq, own_cols + more), BF16)] * nd,
            [
                (0, 0, seq, block_of(s, 0, own_cols), own_cols, s, 0, 0, None)
                for s in range(nd)
            ]
            + [(1, 0, seq, 0, more, s, 0, own_cols, None) for s in range(nd)],
        )
        got = [dperm(v, s) for s, v in enumerate(sent)]
        return cat([v[:, :own_cols] for v in got]), cat([v[:, own_cols:] for v in got])

    def both_heads(own):
        if not split:
            return own
        other = swap(own)
        other = other.reshape(nd, nc, rows, qf)[:, ::-1].reshape(total, qf)
        return pair(own, other, 1)

    one_cols, heads_own = columns_for(after(normed_one, down_cat), heads_out)
    heads_all = both_heads(heads_own)
    low_cols, mid_grad_all = columns_for(resid_low, lora_mid_grad)
    query_all = both_heads(cat([dperm(query_low, s) for s in range(nd)]))

    step = rows // nt
    kv_blocks = kv_sum.reshape(nc, nt, step, HEAD_WIDTH)
    kv_z = kv_blocks[:, 0]
    for z in range(1, nt):
        kv_z = kv_z + tperm(kv_blocks[:, z].astype(BF16), z).astype(F32)
    kv_z = kv_z.astype(BF16).reshape(nc * step, HEAD_WIDTH)
    gain_pack = jnp.concatenate([gain_one_part, gain_two_part]).astype(BF16)
    gain_pack = gain_pack.reshape(-1, HEAD_WIDTH)
    extra = gain_pack.shape[0]
    kv_t = gather_t(jnp.concatenate([kv_z, gain_pack], axis=0))
    kv_pieces = [kv_t] + [dperm(kv_t, s) for s in range(1, nd)]
    kv_grid = jnp.stack(kv_pieces).reshape(nd, nt, nc * step + extra, HEAD_WIDTH)
    kv_mine = kv_grid[:, :, : nc * step].reshape(nd, nt, nc, step, HEAD_WIDTH)
    kv_mine = kv_mine.transpose(0, 2, 1, 3, 4).reshape(total, HEAD_WIDTH)
    kv_back = swap(kv_mine).reshape(nd, nc, rows, HEAD_WIDTH)[:, ::-1]
    kv_back = kv_back.reshape(total, HEAD_WIDTH)
    key_all, value_all = pick(kv_mine, kv_back), pick(kv_back, kv_mine)
    gain_sum = jnp.sum(kv_grid[:, :, nc * step :].astype(F32), axis=(0, 1))
    gain_sum = gain_sum + swap(gain_sum.astype(BF16)).astype(F32)
    gain_sum = gain_sum.reshape(2, nd * nc, own_cols)
    block = di * nc + ci
    gain_own = lax.dynamic_index_in_dim(gain_sum, block, 1, keepdims=False)

    grad_query = mm_tn(one_cols, query_all)
    grad_key = mm_tn(one_cols, key_all)
    grad_value = mm_tn(one_cols, value_all)
    grad_out = mm_tn(heads_all, low_cols)
    out_a = mm_tn(heads_all, masked(mid_grad_all, seq_loop))
    out_a = lax.dynamic_slice_in_dim(out_a, block * a_rows, a_rows, 0)
    grad_out_a = jnp.stack([out_a[:, l * rank : (l + 1) * rank] for l in range(loops)])
    grad_out_b = mm_tn(masked(lora_mid_all, seq_loop), low_cols).reshape(loops, rank, own_cols)
    return (
        outputs,
        input_grad,
        gain_own[0],
        grad_query,
        grad_key,
        grad_value,
        grad_out,
        grad_out_a,
        grad_out_b,
        gain_own[1],
        grad_gate,
        grad_up,
        grad_down,
        grad_down_a,
        grad_down_b,
    )


def solution(mesh):
    both = ("dp", "ctx")
    every = ("tensor", "dp", "ctx")
    params = (
        P(both),
        P(both, "tensor"),
        P(both, None),
        P(both, None),
        P("tensor", both),
        P(None, every, None),
        P(None, None, both),
        P(both),
        P(both, "tensor"),
        P(both, "tensor"),
        P("tensor", both),
        P(None, every, None),
        P(None, None, both),
    )
    rows = (P(both, None), P(both, None))

    return jax.shard_map(
        body,
        mesh=mesh,
        in_specs=rows + (P("dp"),) + params,
        out_specs=rows + params,
        check_vma=False,
    )
```

time: 1840 us -> 625 us (0.34)
  waiting for transfers between devices: 1510 us -> 267 us
  starting transfers between devices: 1.43 us -> 140 us
  matrix products: 179 us -> 61.6 us
  blocking collectives: 104 us -> 0 us
  Pallas kernels: 0 us -> 67.2 us
  local copies, waits for them, and re-layouts: 16.1 us -> 41.1 us
  other arithmetic: 10.1 us -> 33.9 us
    reduce_scatter x12 -> x0, waiting for transfers between devices: 977 us -> none  [the longest x1 210 us: body(): lax.psum_scatter(up_grad_w, ('dp', 'ctx'), scatter_dimension=0, tiled=True)]
    all_gather x10 -> x0, waiting for transfers between devices: 378 us -> none  [the longest x1 88.2 us: body(): lax.all_gather(up_weight, ('dp', 'ctx'), axis=0, tiled=True)]
    ppermute x0 -> x136, waiting for transfers between devices: none -> 267 us  [the longest x55 165 us: dperm(): lax.ppermute(value, 'dp', [(i, i ^ s) for i in range(nd)])]
    psum x3 -> x0, waiting for transfers between devices: 145 us -> none  [the longest x1 54.9 us: body(): lax.psum((attention_part, lowrank_portion), 'tensor')]
    ppermute x0 -> x136, starting transfers between devices: none -> 140 us  [the longest x55 63.8 us: dperm(): lax.ppermute(value, 'dp', [(i, i ^ s) for i in range(nd)])]
    dot_general x39 -> x31, matrix products: 179 us -> 61.6 us  [dot(): lax.dot_general(left, right, (dims, ((), ())), preferred_element_type=F32)]
    pallas_call x0 -> x18, Pallas kernels: none -> 67.2 us  [shuffle(): pl.pallas_call(kernel, out_shape=tuple(outs), in_specs=[pl.BlockSpec(memo...]
    psum x2 -> x0, blocking collectives: 47.3 us -> none  [the longest x1 25.8 us: body(): mlp_sum, mid_sum = lax.psum((mlp_part, mid_part), 'tensor')]
  transfers between devices with their start and end apart: 26 -> 136, of which waited for: 22 -> 51; matrix products, arithmetic and copies ran while one was open for 8% -> 13% of each run, Pallas kernels for 0% -> 8%
where the time goes in v1:
time: 625 us; the launch traced here: 615 us
  waiting for transfers between devices  267 us (43%)
  starting transfers between devices  140 us (22%)
  Pallas kernels  67.2 us (11%)
  matrix products  61.6 us (10%)
  local copies, waits for them, and re-layouts  41.1 us (7%)
  other arithmetic  33.9 us (5%)
    ppermute x55, waiting for transfers between devices, dperm(): lax.ppermute(value, 'dp', [(i, i ^ s) for i in range(nd)])  165 us
    ppermute x36, waiting for transfers between devices, tperm(): return lax.ppermute(value, 'tensor', [(i, i ^ s) for i in range(nt)])  70.7 us
    pallas_call x18, Pallas kernels, shuffle(): pl.pallas_call(kernel, out_shape=tuple(outs), in_specs=[pl.BlockSpec(memo...  67.2 us
    ppermute x55, starting transfers between devices, dperm(): lax.ppermute(value, 'dp', [(i, i ^ s) for i in range(nd)])  63.8 us
    dot_general x31, matrix products, dot(): lax.dot_general(left, right, (dims, ((), ())), preferred_element_type=F32)  61.6 us
    ppermute x36, starting transfers between devices, tperm(): return lax.ppermute(value, 'tensor', [(i, i ^ s) for i in range(nt)])  59.4 us
    ppermute x12, waiting for transfers between devices, send(): return lax.ppermute(value, ('dp', 'ctx'), pairs)  27.2 us
    unnamed x352, local copies, waits for them, and re-layouts  17.7 us
  transfers between devices with their start and end apart: 136, of which 51 were waited for; matrix products, arithmetic and copies ran while one was open for 13% of the time, Pallas kernels for 8%

profile of v1, /device:TPU:0, one launch (start us, length us, event | category | flops | bytes accessed | tf_op | source)
XLA Modules:
  0.0 614.9 jit_solution(4885212514826792123)
XLA Ops:
  15.8 6.7 %collective-permute-done.4.refs_5_ = bf16[272,512]{1,0:T(8,128)(2,1)S(1)} collective-permute-done((bf16[272,512]{1,0:T(8,128)(2,1)S(1)}, bf16[272,512]{1,0:T(8,128)(2,1)S(1)}, u32[]{:S(2)}, u32[]{:S(2)}) %collective-permute-start.4) | collective-permute-done | bytes 278560 | tf_op jit(solution)/shard_map/ppermute | solution.py:141
  50.7 4.8 collective-permute-done.15.refs_7_
  55.5 5.3 collective-permute-done.13.refs_5_
  61.7 5.2 collective-permute-done.11.refs_2_
  84.6 4.7 shard_map.276
  107.1 5.6 collective-permute-done.25
  116.2 12.4 %collective-permute-done.46.refs_1_ = bf16[128,2048]{1,0:T(8,128)(2,1)} collective-permute-done((bf16[128,2048]{1,0:T(8,128)(2,1)S(1)}, bf16[128,2048]{1,0:T(8,128)(2,1)}, u32[]{:S(2)}, u32[]{:S(2)}) %collective-permute-start.46) | collective-permute-done | bytes 524320 | tf_op jit(solution)/shard_map/ppermute | solution.py:144
  128.6 21.0 %collective-permute-done.47.refs_2_ = bf16[128,2048]{1,0:T(8,128)(2,1)S(1)} collective-permute-done((bf16[128,2048]{1,0:T(8,128)(2,1)S(1)}, bf16[128,2048]{1,0:T(8,128)(2,1)S(1)}, u32[]{:S(2)}, u32[]{:S(2)}) %collective-permute-start.47) | collective-permute-done | bytes 524320 | tf_op jit(solution)/shard_map/ppermute | solution.py:144
  162.2 7.8 %collective-permute-done.36.refs_1_ = bf16[256,1024]{1,0:T(8,128)(2,1)S(1)} collective-permute-done((bf16[256,1024]{1,0:T(8,128)(2,1)}, bf16[256,1024]{1,0:T(8,128)(2,1)S(1)}, u32[]{:S(2)}, u32[]{:S(2)}) %collective-permute-start.36) | collective-permute-done | bytes 524320 | tf_op jit(solution)/shard_map/ppermute | solution.py:141
  170.8 6.6 %collective-permute-done.53 = bf16[128,256]{1,0:T(8,128)(2,1)S(1)} collective-permute-done((bf16[128,256]{1,0:T(8,128)(2,1)S(1)}, bf16[128,256]{1,0:T(8,128)(2,1)S(1)}, u32[]{:S(2)}, u32[]{:S(2)}) %collective-permute-start.53) | collective-permute-done | bytes 65568 | tf_op jit(solution)/shard_map/ppermute | solution.py:141
  182.3 23.3 %collective-permute-done.37.refs_2_ = bf16[256,1024]{1,0:T(8,128)(2,1)S(1)} collective-permute-done((bf16[256,1024]{1,0:T(8,128)(2,1)}, bf16[256,1024]{1,0:T(8,128)(2,1)S(1)}, u32[]{:S(2)}, u32[]{:S(2)}) %collective-permute-start.37) | collective-permute-done | bytes 524320 | tf_op jit(solution)/shard_map/ppermute | solution.py:141
  207.5 22.3 %collective-permute-done.41.refs_6_ = bf16[256,1024]{1,0:T(8,128)(2,1)S(1)} collective-permute-done((bf16[256,1024]{1,0:T(8,128)(2,1)}, bf16[256,1024]{1,0:T(8,128)(2,1)S(1)}, u32[]{:S(2)}, u32[]{:S(2)}) %collective-permute-start.41) | collective-permute-done | bytes 524320 | tf_op jit(solution)/shard_map/ppermute | solution.py:152
  239.2 5.3 collective-permute-done.59.refs_3_
  257.1 5.4 shard_map.278.refs_0_
  268.2 4.9 shard_map.275
  273.2 7.9 %fusion.183 = f32[1024,1024]{0,1:T(8,128)S(1)} fusion(bf16[1024,2048]{1,0:T(8,128)(2,1)} %get-tuple-element.118, bf16[2048,1024]{1,0:T(8,128)(2,1)} %shard_map.277), kind=kOutput, calls=%fused_computation.350 | convolution fusion | flops 4294967296 | bytes 12582912 | tf_op jit(solution)/shard_map/dot_general | solution.py:15
  281.1 7.7 %fusion.8 = (bf16[1024,512]{0,1:T(8,128)(2,1)S(1)}, bf16[1024,512]{0,1:T(8,128)(2,1)S(1)}, bf16[1024,512]{0,1:T(8,128)(2,1)}) fusion(f32[1024,1024]{0,1:T(8,128)S(1)} %fusion.183, bf16[1024,2560]{1,0:T(8,128)(2,1)} %shard_map.278.refs_0_, bf16[512,2560]{1,0:T(8,128)(2,1)S(1)} %copy-done.1), kind=kOutput, calls=%fused_computation.27 | convolution fusion | flops 2697461760 | bytes 15204352 | tf_op jit(solution)/shard_map/dot_general | solution.py:15
  305.6 6.8 %collective-permute-done.107 = bf16[256,512]{1,0:T(8,128)(2,1)S(1)} collective-permute-done((bf16[256,512]{1,0:T(8,128)(2,1)}, bf16[256,512]{1,0:T(8,128)(2,1)S(1)}, u32[]{:S(2)}, u32[]{:S(2)}) %collective-permute-start.107) | collective-permute-done | bytes 262176 | tf_op jit(solution)/shard_map/ppermute | solution.py:141
  322.5 7.6 %fusion.159 = (bf16[512,2048]{1,0:T(8,128)(2,1)S(1)}, f32[512,2048]{1,0:T(8,128)}) fusion(bf16[512,2048]{1,0:T(8,128)(2,1)} %collective-permute-done.65, bf16[2048,1024]{1,0:T(8,128)(2,1)} %shard_map.277, bf16[1024,512]{0,1:T(8,128)(2,1)} %copy-done.26, bf16[1024,512]{0,1:T(8,128)(2,1)} %copy-done.27), kind=kOutput, calls=%fused_computation.326 | convolution fusion | flops 2152726528 | bytes 14680064 | tf_op jit(solution)/shard_map/dot_general | solution.py:15
  343.8 5.4 shard_map.286
  349.2 7.6 %convolution_convert_fusion = bf16[2048,1024]{1,0:T(8,128)(2,1)S(1)} fusion(bf16[1024,2048]{1,0:T(8,128)(2,1)} %get-tuple-element.118, bf16[1024,1024]{0,1:T(8,128)(2,1)} %pad_maximum_fusion), kind=kOutput, calls=%fused_computation.3 | convolution fusion | flops 4297064448 | bytes 10485760 | tf_op jit(solution)/shard_map/dot_general | solution.py:15
  356.8 7.5 %collective-permute-done.68 = bf16[128,2048]{1,0:T(8,128)(2,1)} collective-permute-done((bf16[128,2048]{1,0:T(8,128)(2,1)S(1)}, bf16[128,2048]{1,0:T(8,128)(2,1)}, u32[]{:S(2)}, u32[]{:S(2)}) %collective-permute-start.68) | collective-permute-done | bytes 524320 | tf_op jit(solution)/shard_map/ppermute | solution.py:141
  366.2 6.3 %collective-permute-start.70 = (bf16[32,2048]{1,0:T(8,128)(2,1)S(1)}, bf16[32,2048]{1,0:T(8,128)(2,1)S(1)}, u32[]{:S(2)}, u32[]{:S(2)}) collective-permute-start(bf16[32,2048]{1,0:T(8,128)(2,1)S(1)} %get-tuple-element.262), channel_id=1, source_target_pairs={{0,8},{8,0},{16,24},{24,16},{1,9},{9,1},{17,25},{25,17},{2,10},{10... | collective-permute-start | bytes 393224 | tf_op jit(solution)/shard_map/ppermute | solution.py:144
  377.2 7.9 %collective-permute-done.71 = bf16[32,2048]{1,0:T(8,128)(2,1)S(1)} collective-permute-done((bf16[32,2048]{1,0:T(8,128)(2,1)S(1)}, bf16[32,2048]{1,0:T(8,128)(2,1)S(1)}, u32[]{:S(2)}, u32[]{:S(2)}) %collective-permute-start.71) | collective-permute-done | bytes 131104 | tf_op jit(solution)/shard_map/ppermute | solution.py:144
  394.1 6.9 %collective-permute-done.74 = bf16[32,2048]{1,0:T(8,128)(2,1)S(1)} collective-permute-done((bf16[32,2048]{1,0:T(8,128)(2,1)S(1)}, bf16[32,2048]{1,0:T(8,128)(2,1)S(1)}, u32[]{:S(2)}, u32[]{:S(2)}) %collective-permute-start.74) | collective-permute-done | bytes 131104 | tf_op jit(solution)/shard_map/ppermute | solution.py:144
  430.1 8.0 %collective-permute-done.116 = bf16[256,512]{1,0:T(8,128)(2,1)S(1)} collective-permute-done((bf16[256,512]{1,0:T(8,128)(2,1)S(1)}, bf16[256,512]{1,0:T(8,128)(2,1)S(1)}, u32[]{:S(2)}, u32[]{:S(2)}) %collective-permute-start.116) | collective-permute-done | bytes 262176 | tf_op jit(solution)/shard_map/ppermute | solution.py:141
  492.6 7.7 %collective-permute-done.69 = bf16[128,2304]{1,0:T(8,128)(2,1)S(1)} collective-permute-done((bf16[128,2304]{1,0:T(8,128)(2,1)}, bf16[128,2304]{1,0:T(8,128)(2,1)S(1)}, u32[]{:S(2)}, u32[]{:S(2)}) %collective-permute-start.69) | collective-permute-done | bytes 589856 | tf_op jit(solution)/shard_map/ppermute | solution.py:141
  500.2 12.4 %collective-permute-done.78 = bf16[128,2304]{1,0:T(8,128)(2,1)S(1)} collective-permute-done((bf16[128,2304]{1,0:T(8,128)(2,1)}, bf16[128,2304]{1,0:T(8,128)(2,1)S(1)}, u32[]{:S(2)}, u32[]{:S(2)}) %collective-permute-start.78) | collective-permute-done | bytes 589856 | tf_op jit(solution)/shard_map/ppermute | solution.py:141
  535.2 13.7 %collective-permute-done.134 = bf16[128,256]{1,0:T(8,128)(2,1)S(1)} collective-permute-done((bf16[128,256]{1,0:T(8,128)(2,1)S(1)}, bf16[128,256]{1,0:T(8,128)(2,1)S(1)}, u32[]{:S(2)}, u32[]{:S(2)}) %collective-permute-start.134) | collective-permute-done | bytes 65568 | tf_op jit(solution)/shard_map/ppermute | solution.py:141
  585.1 13.0 %collective-permute-done.120.refs_3_ = bf16[256,1024]{1,0:T(8,128)(2,1)S(1)} collective-permute-done((bf16[256,1024]{1,0:T(8,128)(2,1)}, bf16[256,1024]{1,0:T(8,128)(2,1)S(1)}, u32[]{:S(2)}, u32[]{:S(2)}) %collective-permute-start.120) | collective-permute-done | bytes 524320 | tf_op jit(solution)/shard_map/ppermute | solution.py:141
  598.0 9.5 %collective-permute-done.119.refs_2_ = bf16[256,1024]{1,0:T(8,128)(2,1)} collective-permute-done((bf16[256,1024]{1,0:T(8,128)(2,1)}, bf16[256,1024]{1,0:T(8,128)(2,1)}, u32[]{:S(2)}, u32[]{:S(2)}) %collective-permute-start.119) | collective-permute-done | bytes 524320 | tf_op jit(solution)/shard_map/ppermute | solution.py:141
  608.4 6.3 %shard_map.285 = (f32[256,4096]{1,0:T(8,128)}, f32[256,4096]{1,0:T(8,128)}) custom-call(s32[7]{0:T(128)} %pad_add_fusion.2.scalar_ref, bf16[256,1024]{1,0:T(8,128)(2,1)} %get-tuple-element.227.refs_0_, bf16[256,1024]{1,0:T(8,128)(2,1)} %collective-permute-done.118.refs_1_, bf16[256,1024]{1,0:T(8,128)(2,1)} %collective-permute-done.119.refs_2_, ...), custom_call_target="tpu_custom_call" | custom-call | bytes 12582912 | tf_op jit(solution)/shard_map/pallas_call | solution.py:91
  (768 shorter events, 327.3 us)
Async XLA Ops:
  102.9 25.7 %collective-permute-start.46 = (bf16[128,2048]{1,0:T(8,128)(2,1)S(1)}, bf16[128,2048]{1,0:T(8,128)(2,1)}, u32[]{:S(2)}, u32[]{:S(2)}) collective-permute-start(bf16[128,2048]{1,0:T(8,128)(2,1)S(1)} %pad_maximum_fusion.7.refs_0_), channel_id=1, source_target_pairs={{0,8},{8,0},{16,24},{24,16},{1,9},{9,1},{17,25},{25,17},{2,10},{10... | collective-permute-start | bytes 1572872 | tf_op jit(solution)/shard_map/ppermute | solution.py:144
  105.1 44.5 %collective-permute-start.47 = (bf16[128,2048]{1,0:T(8,128)(2,1)S(1)}, bf16[128,2048]{1,0:T(8,128)(2,1)S(1)}, u32[]{:S(2)}, u32[]{:S(2)}) collective-permute-start(bf16[128,2048]{1,0:T(8,128)(2,1)S(1)} %pad_maximum_fusion.7.refs_0_), channel_id=1, source_target_pairs={{0,16},{8,24},{16,0},{24,8},{1,17},{9,25},{17,1},{25,9},{2,18},{10... | collective-permute-start | bytes 1572872 | tf_op jit(solution)/shard_map/ppermute | solution.py:144
  112.9 41.6 %collective-permute-start.27 = (bf16[128,2304]{1,0:T(8,128)(2,1)S(1)}, bf16[128,2304]{1,0:T(8,128)(2,1)}, u32[]{:S(2)}, u32[]{:S(2)}) collective-permute-start(bf16[128,2304]{1,0:T(8,128)(2,1)S(1)} %pad_maximum_fusion.3.refs_0_), channel_id=1, source_target_pairs={{0,2},{2,0},{4,6},{6,4},{1,3},{3,1},{5,7},{7,5},{8,10},{10,8},{12,... | collective-permute-start | bytes 1769480 | tf_op jit(solution)/shard_map/ppermute | solution.py:141
  113.5 41.4 %collective-permute-start.28 = (bf16[128,2304]{1,0:T(8,128)(2,1)S(1)}, bf16[128,2304]{1,0:T(8,128)(2,1)}, u32[]{:S(2)}, u32[]{:S(2)}) collective-permute-start(bf16[128,2304]{1,0:T(8,128)(2,1)S(1)} %pad_maximum_fusion.3.refs_0_), channel_id=1, source_target_pairs={{0,4},{2,6},{4,0},{6,2},{1,5},{3,7},{5,1},{7,3},{8,12},{10,14},{12... | collective-permute-start | bytes 1769480 | tf_op jit(solution)/shard_map/ppermute | solution.py:141
  114.4 39.4 %collective-permute-start.48 = (bf16[128,2048]{1,0:T(8,128)(2,1)S(1)}, bf16[128,2048]{1,0:T(8,128)(2,1)}, u32[]{:S(2)}, u32[]{:S(2)}) collective-permute-start(bf16[128,2048]{1,0:T(8,128)(2,1)S(1)} %pad_maximum_fusion.7.refs_0_), channel_id=1, source_target_pairs={{0,24},{8,16},{16,8},{24,0},{1,25},{9,17},{17,9},{25,1},{2,26},{10... | collective-permute-start | bytes 1572872 | tf_op jit(solution)/shard_map/ppermute | solution.py:144
  128.6 25.8 %collective-permute-start.49 = (bf16[128,2048]{1,0:T(8,128)(2,1)S(1)}, bf16[128,2048]{1,0:T(8,128)(2,1)}, u32[]{:S(2)}, u32[]{:S(2)}) collective-permute-start(bf16[128,2048]{1,0:T(8,128)(2,1)S(1)} %pad_maximum_fusion.7.refs_0_), channel_id=1, source_target_pairs={{0,1},{1,0},{2,3},{3,2},{4,5},{5,4},{6,7},{7,6},{8,9},{9,8},{10,11... | collective-permute-start | bytes 1572872 | tf_op jit(solution)/shard_map/ppermute | solution.py:138
  157.5 22.0 %collective-permute-start.29 = (bf16[64,2304]{1,0:T(8,128)(2,1)S(1)}, bf16[64,2304]{1,0:T(8,128)(2,1)}, u32[]{:S(2)}, u32[]{:S(2)}) collective-permute-start(bf16[64,2304]{1,0:T(8,128)(2,1)S(1)} %slice.555), channel_id=1, source_target_pairs={{0,4},{2,6},{4,0},{6,2},{1,5},{3,7},{5,1},{7,3},{8,12},{10,14},{12... | collective-permute-start | bytes 884744 | tf_op jit(solution)/shard_map/ppermute | solution.py:141
  158.4 23.2 %collective-permute-start.30 = (bf16[64,2304]{1,0:T(8,128)(2,1)S(1)}, bf16[64,2304]{1,0:T(8,128)(2,1)}, u32[]{:S(2)}, u32[]{:S(2)}) collective-permute-start(bf16[64,2304]{1,0:T(8,128)(2,1)S(1)} %slice.556), channel_id=1, source_target_pairs={{0,2},{2,0},{4,6},{6,4},{1,3},{3,1},{5,7},{7,5},{8,10},{10,8},{12,... | collective-permute-start | bytes 884744 | tf_op jit(solution)/shard_map/ppermute | solution.py:141
  177.5 28.1 %collective-permute-start.37 = (bf16[256,1024]{1,0:T(8,128)(2,1)}, bf16[256,1024]{1,0:T(8,128)(2,1)S(1)}, u32[]{:S(2)}, u32[]{:S(2)}) collective-permute-start(bf16[256,1024]{1,0:T(8,128)(2,1)} %get-tuple-element.126), channel_id=1, source_target_pairs={{0,4},{2,6},{4,0},{6,2},{1,5},{3,7},{5,1},{7,3},{8,12},{10,14},{12... | collective-permute-start | bytes 1572872 | tf_op jit(solution)/shard_map/ppermute | solution.py:141
  178.4 27.2 %collective-permute-start.38 = (bf16[256,1024]{1,0:T(8,128)(2,1)}, bf16[256,1024]{1,0:T(8,128)(2,1)S(1)}, u32[]{:S(2)}, u32[]{:S(2)}) collective-permute-start(bf16[256,1024]{1,0:T(8,128)(2,1)} %get-tuple-element.129), channel_id=1, source_target_pairs={{0,6},{2,4},{4,2},{6,0},{1,7},{3,5},{5,3},{7,1},{8,14},{10,12},{12... | collective-permute-start | bytes 1572872 | tf_op jit(solution)/shard_map/ppermute | solution.py:141
  179.5 27.4 %collective-permute-start.40 = (bf16[256,1024]{1,0:T(8,128)(2,1)}, bf16[256,1024]{1,0:T(8,128)(2,1)S(1)}, u32[]{:S(2)}, u32[]{:S(2)}) collective-permute-start(bf16[256,1024]{1,0:T(8,128)(2,1)} %get-tuple-element.134), channel_id=1, source_target_pairs={{0,3},{1,2},{2,1},{3,0},{4,7},{5,6},{6,5},{7,4},{8,11},{9,10},{10,... | collective-permute-start | bytes 1572872 | tf_op jit(solution)/shard_map/ppermute | solution.py:152
  179.5 50.3 %collective-permute-start.41 = (bf16[256,1024]{1,0:T(8,128)(2,1)}, bf16[256,1024]{1,0:T(8,128)(2,1)S(1)}, u32[]{:S(2)}, u32[]{:S(2)}) collective-permute-start(bf16[256,1024]{1,0:T(8,128)(2,1)} %get-tuple-element.137), channel_id=1, source_target_pairs={{0,5},{1,4},{2,7},{3,6},{4,1},{5,0},{6,3},{7,2},{8,13},{9,12},{10,... | collective-permute-start | bytes 1572872 | tf_op jit(solution)/shard_map/ppermute | solution.py:152
  181.6 49.8 %collective-permute-start.42 = (bf16[256,1024]{1,0:T(8,128)(2,1)}, bf16[256,1024]{1,0:T(8,128)(2,1)S(1)}, u32[]{:S(2)}, u32[]{:S(2)}) collective-permute-start(bf16[256,1024]{1,0:T(8,128)(2,1)} %get-tuple-element.140), channel_id=1, source_target_pairs={{0,7},{1,6},{2,5},{3,4},{4,3},{5,2},{6,1},{7,0},{8,15},{9,14},{10,... | collective-permute-start | bytes 1572872 | tf_op jit(solution)/shard_map/ppermute | solution.py:152
  205.6 27.9 %collective-permute-start.56 = (bf16[512,256]{1,0:T(8,128)(2,1)S(1)}, bf16[512,256]{1,0:T(8,128)(2,1)S(1)}, u32[]{:S(2)}, u32[]{:S(2)}) collective-permute-start(bf16[512,256]{1,0:T(8,128)(2,1)S(1)} %pad_maximum_fusion.19.refs_8_), channel_id=1, source_target_pairs={{0,1},{1,0},{2,3},{3,2},{4,5},{5,4},{6,7},{7,6},{8,9},{9,8},{10,11... | collective-permute-start | bytes 786440 | tf_op jit(solution)/shard_map/ppermute | solution.py:138
  205.6 27.9 %collective-permute-start.63 = (bf16[512,256]{1,0:T(8,128)(2,1)S(1)}, bf16[512,256]{1,0:T(8,128)(2,1)S(1)}, u32[]{:S(2)}, u32[]{:S(2)}) collective-permute-start(bf16[512,256]{1,0:T(8,128)(2,1)S(1)} %copy-done.157), channel_id=1, source_target_pairs={{0,7},{1,6},{2,5},{3,4},{4,3},{5,2},{6,1},{7,0},{8,15},{9,14},{10,... | collective-permute-start | bytes 786440 | tf_op jit(solution)/shard_map/ppermute | solution.py:152
  206.9 27.2 %collective-permute-start.62 = (bf16[512,256]{1,0:T(8,128)(2,1)S(1)}, bf16[512,256]{1,0:T(8,128)(2,1)S(1)}, u32[]{:S(2)}, u32[]{:S(2)}) collective-permute-start(bf16[512,256]{1,0:T(8,128)(2,1)S(1)} %copy-done.156), channel_id=1, source_target_pairs={{0,5},{1,4},{2,7},{3,6},{4,1},{5,0},{6,3},{7,2},{8,13},{9,12},{10,... | collective-permute-start | bytes 786440 | tf_op jit(solution)/shard_map/ppermute | solution.py:152
  233.5 32.8 %collective-permute-start.31 = (bf16[128,2304]{1,0:T(8,128)(2,1)S(1)}, bf16[128,2304]{1,0:T(8,128)(2,1)S(1)}, u32[]{:S(2)}, u32[]{:S(2)}) collective-permute-start(bf16[128,2304]{1,0:T(8,128)(2,1)S(1)} %pad_maximum_fusion.3.refs_0_), channel_id=1, source_target_pairs={{0,1},{1,0},{2,3},{3,2},{4,5},{5,4},{6,7},{7,6},{8,9},{9,8},{10,11... | collective-permute-start | bytes 1769480 | tf_op jit(solution)/shard_map/ppermute | solution.py:138
  233.6 32.7 %collective-permute-start.32 = (bf16[128,2304]{1,0:T(8,128)(2,1)}, bf16[128,2304]{1,0:T(8,128)(2,1)S(1)}, u32[]{:S(2)}, u32[]{:S(2)}) collective-permute-start(bf16[128,2304]{1,0:T(8,128)(2,1)} %collective-permute-done.27.refs_1_), channel_id=1, source_target_pairs={{0,1},{1,0},{2,3},{3,2},{4,5},{5,4},{6,7},{7,6},{8,9},{9,8},{10,11... | collective-permute-start | bytes 1769480 | tf_op jit(solution)/shard_map/ppermute | solution.py:138
  234.1 32.2 %collective-permute-start.33 = (bf16[128,2304]{1,0:T(8,128)(2,1)}, bf16[128,2304]{1,0:T(8,128)(2,1)S(1)}, u32[]{:S(2)}, u32[]{:S(2)}) collective-permute-start(bf16[128,2304]{1,0:T(8,128)(2,1)} %collective-permute-done.28.refs_2_), channel_id=1, source_target_pairs={{0,1},{1,0},{2,3},{3,2},{4,5},{5,4},{6,7},{7,6},{8,9},{9,8},{10,11... | collective-permute-start | bytes 1769480 | tf_op jit(solution)/shard_map/ppermute | solution.py:138
  292.6 29.9 %collective-permute-start.65 = (bf16[512,2048]{1,0:T(8,128)(2,1)}, bf16[512,2048]{1,0:T(8,128)(2,1)}, u32[]{:S(2)}, u32[]{:S(2)}) collective-permute-start(bf16[512,2048]{1,0:T(8,128)(2,1)} %convolution_convert_fusion.2), channel_id=1, source_target_pairs={{0,1},{1,0},{2,3},{3,2},{4,5},{5,4},{6,7},{7,6},{8,9},{9,8},{10,11... | collective-permute-start | bytes 6291464 | tf_op jit(solution)/shard_map/ppermute | solution.py:138
  339.5 24.8 %collective-permute-start.68 = (bf16[128,2048]{1,0:T(8,128)(2,1)S(1)}, bf16[128,2048]{1,0:T(8,128)(2,1)}, u32[]{:S(2)}, u32[]{:S(2)}) collective-permute-start(bf16[128,2048]{1,0:T(8,128)(2,1)S(1)} %get-tuple-element.232), channel_id=1, source_target_pairs={{0,6},{2,4},{4,2},{6,0},{1,7},{3,5},{5,3},{7,1},{8,14},{10,12},{12... | collective-permute-start | bytes 1572872 | tf_op jit(solution)/shard_map/ppermute | solution.py:141
  343.8 133.8 %collective-permute-start.64 = (bf16[512,2304]{1,0:T(8,128)(2,1)}, bf16[512,2304]{1,0:T(8,128)(2,1)}, u32[]{:S(2)}, u32[]{:S(2)}) collective-permute-start(bf16[512,2304]{1,0:T(8,128)(2,1)} %pad_maximum_fusion.1), channel_id=1, source_target_pairs={{0,1},{1,0},{2,3},{3,2},{4,5},{5,4},{6,7},{7,6},{8,9},{9,8},{10,11... | collective-permute-start | bytes 7077896 | tf_op jit(solution)/shard_map/ppermute | solution.py:138
  429.5 22.1 %collective-permute-start.112 = (bf16[1024,256]{1,0:T(8,128)(2,1)}, bf16[1024,256]{1,0:T(8,128)(2,1)}, u32[]{:S(2)}, u32[]{:S(2)}) collective-permute-start(bf16[1024,256]{1,0:T(8,128)(2,1)} %pad_maximum_fusion.10), channel_id=1, source_target_pairs={{0,1},{1,0},{2,3},{3,2},{4,5},{5,4},{6,7},{7,6},{8,9},{9,8},{10,11... | collective-permute-start | bytes 1572872 | tf_op jit(solution)/shard_map/ppermute | solution.py:138
  484.8 27.8 %collective-permute-start.78 = (bf16[128,2304]{1,0:T(8,128)(2,1)}, bf16[128,2304]{1,0:T(8,128)(2,1)S(1)}, u32[]{:S(2)}, u32[]{:S(2)}) collective-permute-start(bf16[128,2304]{1,0:T(8,128)(2,1)} %get-tuple-element.231), channel_id=1, source_target_pairs={{0,4},{2,6},{4,0},{6,2},{1,5},{3,7},{5,1},{7,3},{8,12},{10,14},{12... | collective-permute-start | bytes 1769480 | tf_op jit(solution)/shard_map/ppermute | solution.py:141
  485.9 26.7 %collective-permute-start.79 = (bf16[128,2304]{1,0:T(8,128)(2,1)}, bf16[128,2304]{1,0:T(8,128)(2,1)S(1)}, u32[]{:S(2)}, u32[]{:S(2)}) collective-permute-start(bf16[128,2304]{1,0:T(8,128)(2,1)} %get-tuple-element.230), channel_id=1, source_target_pairs={{0,6},{2,4},{4,2},{6,0},{1,7},{3,5},{5,3},{7,1},{8,14},{10,12},{12... | collective-permute-start | bytes 1769480 | tf_op jit(solution)/shard_map/ppermute | solution.py:141
  488.6 36.7 %collective-permute-start.128 = (bf16[512,256]{1,0:T(8,128)(2,1)}, bf16[512,256]{1,0:T(8,128)(2,1)S(1)}, u32[]{:S(2)}, u32[]{:S(2)}) collective-permute-start(bf16[512,256]{1,0:T(8,128)(2,1)} %get-tuple-element.191), channel_id=1, source_target_pairs={{0,1},{1,0},{2,3},{3,2},{4,5},{5,4},{6,7},{7,6},{8,9},{9,8},{10,11... | collective-permute-start | bytes 786440 | tf_op jit(solution)/shard_map/ppermute | solution.py:138
  529.6 21.2 %collective-permute-start.130 = (bf16[512,256]{1,0:T(8,128)(2,1)S(1)}, bf16[512,256]{1,0:T(8,128)(2,1)S(1)}, u32[]{:S(2)}, u32[]{:S(2)}) collective-permute-start(bf16[512,256]{1,0:T(8,128)(2,1)S(1)} %copy-done.150), channel_id=1, source_target_pairs={{0,5},{1,4},{2,7},{3,6},{4,1},{5,0},{6,3},{7,2},{8,13},{9,12},{10,... | collective-permute-start | bytes 786440 | tf_op jit(solution)/shard_map/ppermute | solution.py:152
  548.9 27.4 %collective-permute-start.121 = (bf16[256,1024]{1,0:T(8,128)(2,1)S(1)}, bf16[256,1024]{1,0:T(8,128)(2,1)S(1)}, u32[]{:S(2)}, u32[]{:S(2)}) collective-permute-start(bf16[256,1024]{1,0:T(8,128)(2,1)S(1)} %copy-done.67), channel_id=1, source_target_pairs={{0,1},{1,0},{2,3},{3,2},{4,5},{5,4},{6,7},{7,6},{8,9},{9,8},{10,11... | collective-permute-start | bytes 1572872 | tf_op jit(solution)/shard_map/ppermute | solution.py:138
  549.6 29.3 %collective-permute-start.124 = (bf16[256,1024]{1,0:T(8,128)(2,1)}, bf16[256,1024]{1,0:T(8,128)(2,1)S(1)}, u32[]{:S(2)}, u32[]{:S(2)}) collective-permute-start(bf16[256,1024]{1,0:T(8,128)(2,1)} %get-tuple-element.181), channel_id=1, source_target_pairs={{0,7},{1,6},{2,5},{3,4},{4,3},{5,2},{6,1},{7,0},{8,15},{9,14},{10,... | collective-permute-start | bytes 1572872 | tf_op jit(solution)/shard_map/ppermute | solution.py:152
  576.3 21.7 %collective-permute-start.120 = (bf16[256,1024]{1,0:T(8,128)(2,1)}, bf16[256,1024]{1,0:T(8,128)(2,1)S(1)}, u32[]{:S(2)}, u32[]{:S(2)}) collective-permute-start(bf16[256,1024]{1,0:T(8,128)(2,1)} %get-tuple-element.178), channel_id=1, source_target_pairs={{0,6},{2,4},{4,2},{6,0},{1,7},{3,5},{5,3},{7,1},{8,14},{10,12},{12... | collective-permute-start | bytes 1572872 | tf_op jit(solution)/shard_map/ppermute | solution.py:141
  577.9 29.7 %collective-permute-start.119 = (bf16[256,1024]{1,0:T(8,128)(2,1)}, bf16[256,1024]{1,0:T(8,128)(2,1)}, u32[]{:S(2)}, u32[]{:S(2)}) collective-permute-start(bf16[256,1024]{1,0:T(8,128)(2,1)} %get-tuple-element.177), channel_id=1, source_target_pairs={{0,4},{2,6},{4,0},{6,2},{1,5},{3,7},{5,1},{7,3},{8,12},{10,14},{12... | collective-permute-start | bytes 1572872 | tf_op jit(solution)/shard_map/ppermute | solution.py:141
  579.0 29.4 %collective-permute-start.118 = (bf16[256,1024]{1,0:T(8,128)(2,1)}, bf16[256,1024]{1,0:T(8,128)(2,1)}, u32[]{:S(2)}, u32[]{:S(2)}) collective-permute-start(bf16[256,1024]{1,0:T(8,128)(2,1)} %get-tuple-element.176), channel_id=1, source_target_pairs={{0,2},{2,0},{4,6},{6,4},{1,3},{3,1},{5,7},{7,5},{8,10},{10,8},{12,... | collective-permute-start | bytes 1572872 | tf_op jit(solution)/shard_map/ppermute | solution.py:141
  (276 other events, 3780.5 us)
